TPU v7x, 256 devices: a whole 4x4x8 slice. The times are simulated.
256 devices in a mesh: batch: 2 (over x_lo), ctx: 64 (over z, y, core), head: 2 (over x_hi).
Axes of the slice: x: 4 (x_hi: 2, x_lo: 2; x = x_hi * 2 + x_lo), y: 4, z: 8, core: 2. Of those that a mesh axis runs over, the one named last changes fastest.
Arguments:
- stored_keys: bfloat16 [262144, 8, 128], P(('batch', 'ctx'), 'head'), parts along dimension 0, may hold values from -16 to 16
- stored_values: bfloat16 [262144, 8, 128], P(('batch', 'ctx'), 'head'), parts along dimension 0, may hold values from -24 to 24
- observed_queries: bfloat16 [256, 40, 128], P('batch', 'head'), parts along dimension 0, may hold values from -256 to 256
- decoded_queries: bfloat16 [8, 40, 128], P('batch', 'head'), parts along dimension 0, may hold values from -256 to 256
- step_keys: bfloat16 [8, 8, 128], P('batch', 'head'), parts along dimension 0, may hold values from -16 to 16
- decoded_values: bfloat16 [8, 8, 128], P('batch', 'head'), parts along dimension 0, may hold values from -6 to 6
- keep_lists: int32 [128, 26], P(('batch', 'ctx')), parts along dimension 0, may hold values from 0 to 31, as said below
- owner_ids: int32 [128, 26], P(('batch', 'ctx')), parts along dimension 0, may hold values from 0 to 63, as said below
- cache_length: int32 [2], P('batch'), parts along dimension 0, may hold values from 65536 to 131072
Outputs:
- token_scores: float32 [16, 131072], P(('batch', 'head'), 'ctx'), parts along dimension 0
- retained_keys: bfloat16 [212992, 8, 128], P(('batch', 'ctx'), 'head'), parts along dimension 0
- retained_values: bfloat16 [212992, 8, 128], P(('batch', 'ctx'), 'head'), parts along dimension 0
- decoded: bfloat16 [8, 40, 128], P('batch', 'head'), parts along dimension 0
There are 2 independent parts, one for each index of `batch`. A program takes and returns all parts, laid end to end along the dimension named above; each array names one. Nothing has to cross between parts.
Inputs may be any that keep to these rules, and one draw needn't show every extreme that they name: `keep_lists`: each row names 26 distinct blocks among its own 32 blocks, numbered locally. `owner_ids`: each row names any owner at most 1 times and some owner exactly 1 times; every owner is named exactly 26 times in all rows.
All inputs are finite; a program needn't handle non-finite values.
Results may differ from a plain program's by a relative error of at most 0.00155.
The roundings to bfloat16 on the way count: a program that leaves them out, or rounds other values in their place, can miss the bound.
Values may be sent and summed in bfloat16 or wider, within the bound.
A program may use at most 192 MiB of HBM per device.

v0:
```python
import math

import jax
import jax.numpy as jnp
from jax import lax
from jax.sharding import Mesh
from jax.sharding import PartitionSpec as P

BLOCK_TOKENS = 64
CTX = ("ctx_0", "ctx_1", "ctx_2")
BATCH_CTX = ("batch", "ctx_0", "ctx_1", "ctx_2")


MASK_FILL = -1e30
LAMBDA = 0.1
NORM_EPS = 1e-06


def copy_for_each(value, axis):
    length = lax.axis_size(axis)
    return lax.all_to_all(
        jnp.broadcast_to(value[None], (length, *value.shape)), axis, 0, 0, tiled=True
    )


def over_copies(value, axis):
    return copy_for_each(value, axis).max(axis=0)


def of_everyone(value, axis):
    return copy_for_each(value, axis).sum(axis=0)


def in_one(arrays, axis):
    ends = [0]
    for a in arrays:
        ends.append(ends[-1] + a.size)
    running = of_everyone(jnp.concatenate([a.ravel() for a in arrays]), axis)
    return tuple((running[b:e].reshape(a.shape) for a, b, e in zip(arrays, ends, ends[1:])))


def gathered_once(value, axis):
    leaves = jax.tree.leaves(value)
    sequence = sorted(range(len(leaves)), key=lambda k: -leaves[k].size)
    width = (1, *leaves[sequence[0]].shape)[-1]
    lines = [
        jnp.pad(leaves[k].reshape(-1), (0, -leaves[k].size % width)).reshape(-1, width)
        for k in sequence
    ]
    both, at, found = (lax.all_gather(jnp.concatenate(lines), axis), 0, {})
    for k, line in zip(sequence, lines):
        section = both[:, at : at + len(line)].reshape(len(both), -1)
        found[k] = section[:, : leaves[k].size].reshape(-1, *leaves[k].shape)
        at += len(line)
    numbers = iter(range(len(leaves)))
    return jax.tree.map(lambda _: found[next(numbers)], value)


def combined_by_axis(value, axes, combine):
    for axis in axes:
        pieces = gathered_once(value, axis)
        value = jax.tree.map(lambda part: part[0], pieces)
        for k in range(1, lax.axis_size(axis)):
            value = combine(value, jax.tree.map(lambda part: part[k], pieces))
    return value


def merge_stats(earlier_pair, later_pair):
    joint_max = jnp.maximum(earlier_pair[0], later_pair[0])
    joint_sum = earlier_pair[1] * jnp.exp(earlier_pair[0] - joint_max) + later_pair[1] * jnp.exp(
        later_pair[0] - joint_max
    )
    return (joint_max, joint_sum)


def decode_partial(
    queries, block_keys, block_values, block_live, new_keys, new_values, logit_scale
):
    step_count = queries.shape[0]
    cache_logits = (
        jnp.einsum("sgrd,ngd->sgrn", queries, block_keys, preferred_element_type=jnp.float32)
        * logit_scale
    )
    new_logits = (
        jnp.einsum("sgrd,ugd->sgru", queries, new_keys, preferred_element_type=jnp.float32)
        * logit_scale
    )
    causal = (
        jnp.arange(step_count, dtype=jnp.int32)[:, None]
        >= jnp.arange(step_count, dtype=jnp.int32)[None, :]
    )
    causal_bcast = causal[:, None, None, :]
    live_bcast = block_live[None, None, None, :]
    local_top = jnp.maximum(
        jnp.max(jnp.where(live_bcast, cache_logits, MASK_FILL), axis=3),
        jnp.max(jnp.where(causal_bcast, new_logits, MASK_FILL), axis=3),
    )
    row_max = over_copies(local_top, CTX)
    cache_exp = jnp.where(live_bcast, jnp.exp(cache_logits - row_max[..., None]), 0.0)
    cache_weighted = jnp.einsum(
        "sgrn,ngd->sgrd",
        cache_exp.astype(jnp.bfloat16),
        block_values,
        preferred_element_type=jnp.float32,
    )
    weighted, denominator = in_one((cache_weighted, jnp.sum(cache_exp, axis=3)), CTX)
    new_exp = jnp.where(causal_bcast, jnp.exp(new_logits - row_max[..., None]), 0.0)
    weighted = weighted + jnp.einsum(
        "sgru,ugd->sgrd",
        new_exp.astype(jnp.bfloat16),
        new_values,
        preferred_element_type=jnp.float32,
    )
    denominator = denominator + jnp.sum(new_exp, axis=3)
    return weighted / denominator[..., None]


def shards(
    stored_keys,
    stored_values,
    observed_queries,
    decoded_queries,
    step_keys,
    decoded_values,
    keep_lists,
    owner_ids,
    cache_length,
):
    highest = lax.Precision.HIGHEST
    ctx_count = lax.axis_size(CTX)
    ctx_rank = lax.axis_index(CTX)
    tokens, head_count, head_width = stored_keys.shape
    window_rows = observed_queries.shape[0]
    group_size = observed_queries.shape[1] // head_count
    step_count = decoded_queries.shape[0]
    blocks_here = tokens // BLOCK_TOKENS
    kept_count = keep_lists.shape[1]
    logit_scale = 1.0 / math.sqrt(head_width)
    seq_length = cache_length[0]
    positions = ctx_rank * tokens + jnp.arange(tokens, dtype=jnp.int32)
    is_live = positions < seq_length
    live_mask = is_live[None, :]
    grouped = observed_queries.reshape(window_rows, head_count, group_size, head_width)
    logit_list = []
    for head_index in range(head_count):
        product = jnp.einsum(
            "wrd,td->wrt",
            grouped[:, head_index],
            stored_keys[:, head_index],
            preferred_element_type=jnp.float32,
        )
        logit_list.append(product.reshape(window_rows * group_size, tokens) * logit_scale)
    local_max = jnp.stack(
        [jnp.max(jnp.where(live_mask, logit_rows, MASK_FILL), axis=1) for logit_rows in logit_list]
    )
    exp_list = [
        jnp.where(live_mask, jnp.exp(logit_list[head_index] - local_max[head_index][:, None]), 0.0)
        for head_index in range(head_count)
    ]
    local_sum = jnp.stack([jnp.sum(exp_rows, axis=1) for exp_rows in exp_list])
    row_max, row_sum = combined_by_axis((local_max, local_sum), CTX, merge_stats)
    rescale = jnp.exp(local_max - row_max) / row_sum
    weight_sum = jnp.stack(
        [
            jnp.sum(exp_list[head_index] * rescale[head_index][:, None], axis=0)
            for head_index in range(head_count)
        ]
    )
    importance = weight_sum * (seq_length.astype(jnp.float32) / (window_rows * group_size))
    blocked_keys = stored_keys.reshape(blocks_here, BLOCK_TOKENS, head_count, head_width)
    value_blocks = stored_values.reshape(blocks_here, BLOCK_TOKENS, head_count, head_width)
    live_blocks = is_live.astype(jnp.float32).reshape(blocks_here, BLOCK_TOKENS)
    gram_matrix = jnp.einsum(
        "bigd,bjgd->bgij", blocked_keys, blocked_keys, preferred_element_type=jnp.float32
    )
    diagonal = jnp.diagonal(gram_matrix, axis1=2, axis2=3)
    key_norms = jnp.sqrt(diagonal + NORM_EPS)
    spread = live_blocks[:, None, :] / key_norms
    rowsum = jnp.einsum("bgij,bgj->bgi", gram_matrix, spread, precision=highest) / key_norms
    own_term = live_blocks[:, None, :] * diagonal / (key_norms * key_norms)
    counts = jnp.sum(live_blocks, axis=1)
    redundancy_score = (rowsum - own_term) / jnp.maximum(counts - 1.0, 1.0)[:, None, None]
    redundancy_score = redundancy_score.transpose(1, 0, 2).reshape(head_count, tokens)
    token_scores = jnp.where(
        live_mask, LAMBDA * importance - (1.0 - LAMBDA) * redundancy_score, 0.0
    )
    keep_row = keep_lists[0]
    owner_row = owner_ids[0]
    capacity = (kept_count + ctx_count - 1) // ctx_count
    slot_total = ctx_count * capacity
    kept_range = jnp.arange(kept_count, dtype=jnp.int32)
    same_owner = owner_row[None, :] == owner_row[:, None]
    before = kept_range[None, :] < kept_range[:, None]
    earlier = jnp.sum((same_owner & before).astype(jnp.int32), axis=1)
    slot_of = owner_row * capacity + earlier
    slot_match = slot_of[None, :] == jnp.arange(slot_total, dtype=jnp.int32)[:, None]
    slot_used = jnp.any(slot_match, axis=1)
    slot_source = jnp.sum(slot_match.astype(jnp.int32) * kept_range[None, :], axis=1)
    slot_block = jnp.take(keep_row, slot_source)
    used_mask = slot_used[:, None, None, None]
    send_keys = jnp.where(used_mask, blocked_keys[slot_block], jnp.zeros((), jnp.bfloat16))
    send_values = jnp.where(used_mask, value_blocks[slot_block], jnp.zeros((), jnp.bfloat16))
    send_live = jnp.where(slot_used[:, None], live_blocks[slot_block], 0.0).astype(jnp.bfloat16)
    send_used = slot_used.astype(jnp.bfloat16)
    got_keys, got_values, got_live, got_used = (
        lax.all_to_all(
            send_keys.reshape(ctx_count, capacity, BLOCK_TOKENS, head_count, head_width),
            CTX,
            split_axis=0,
            concat_axis=0,
            tiled=True,
        ),
        lax.all_to_all(
            send_values.reshape(ctx_count, capacity, BLOCK_TOKENS, head_count, head_width),
            CTX,
            split_axis=0,
            concat_axis=0,
            tiled=True,
        ),
        lax.all_to_all(
            send_live.reshape(ctx_count, capacity, BLOCK_TOKENS),
            CTX,
            split_axis=0,
            concat_axis=0,
            tiled=True,
        ),
        lax.all_to_all(
            send_used.reshape(ctx_count, capacity), CTX, split_axis=0, concat_axis=0, tiled=True
        ),
    )
    recv_keys = got_keys.reshape(slot_total, BLOCK_TOKENS, head_count, head_width)
    recv_values = got_values.reshape(slot_total, BLOCK_TOKENS, head_count, head_width)
    recv_live = got_live.reshape(slot_total, BLOCK_TOKENS)
    used_int = (got_used.reshape(slot_total) > 0.5).astype(jnp.int32)
    slot_rank = jnp.cumsum(used_int) - 1
    pick_match = (slot_rank[None, :] == kept_range[:, None]) & (used_int[None, :] > 0)
    picked = jnp.sum(
        pick_match.astype(jnp.int32) * jnp.arange(slot_total, dtype=jnp.int32)[None, :], axis=1
    )
    retained_keys = recv_keys[picked].reshape(kept_count * BLOCK_TOKENS, head_count, head_width)
    retained_values = recv_values[picked].reshape(kept_count * BLOCK_TOKENS, head_count, head_width)
    kept_live = recv_live[picked].reshape(kept_count * BLOCK_TOKENS) > 0.5
    step_rows = decoded_queries.reshape(step_count, head_count, group_size, head_width)
    attended = decode_partial(
        step_rows, retained_keys, retained_values, kept_live, step_keys, decoded_values, logit_scale
    )
    decoded = attended.reshape(step_count, head_count * group_size, head_width).astype(jnp.bfloat16)
    return (token_scores, retained_keys, retained_values, decoded)


def solution(mesh):
    split = Mesh(
        mesh.devices.reshape(mesh.shape["batch"], 8, 4, 2, mesh.shape["head"]),
        ("batch", "ctx_0", "ctx_1", "ctx_2", "head"),
    )
    return jax.shard_map(
        shards,
        mesh=split,
        in_specs=(
            P(BATCH_CTX, "head", None),
            P(BATCH_CTX, "head", None),
            P("batch", "head", None),
            P("batch", "head", None),
            P("batch", "head", None),
            P("batch", "head", None),
            P(BATCH_CTX, None),
            P(BATCH_CTX, None),
            P("batch"),
        ),
        out_specs=(
            P(("batch", "head"), CTX),
            P(BATCH_CTX, "head", None),
            P(BATCH_CTX, "head", None),
            P("batch", "head", None),
        ),
        check_vma=False,
    )
```

profile of v0, /device:TPU:1, one launch (start us, length us, event | category | flops | bytes accessed | tf_op | source)
XLA Modules:
  0.0 405.7 jit_solution(7165101037131020603)
XLA Ops:
  3.1 13.1 %all-to-all-start.1 = ((bf16[64,1,1]{2,1,0:T(2,128)(2,1)}), bf16[64,1,1]{2,1,0:T(2,128)(2,1)S(1)}, u32[]{:S(2)}, u32[]{:S(2)}) async-start(bf16[64,1,1]{2,1,0:T(2,128)(2,1)} %copy.232), calls=%async_computation.1 | async-start | bytes 65536 | tf_op jit(solution)/shard_map/all_to_all | solution.py:227
  19.3 6.3 %gather_fusion.4 = bf16[64,64,4,128]{3,2,1,0:T(4,128)(2,1)} fusion(bf16[32,64,4,128]{3,2,1,0:T(4,128)(2,1)S(1)} %bitcast.395, s32[1024]{0:T(1024)S(1)} %pad_clamp_fusion.1), kind=kCustom, calls=%fused_computation.4 | custom fusion | bytes 8388864 | tf_op jit(solution)/shard_map/gather | solution.py:202
  25.5 7.9 %gather_fusion.2 = bf16[64,64,4,128]{3,2,1,0:T(4,128)(2,1)} fusion(bf16[32,64,4,128]{3,2,1,0:T(4,128)(2,1)} %bitcast.397, s32[1024]{0:T(1024)S(1)} %pad_clamp_fusion.1), kind=kCustom, calls=%fused_computation.2 | custom fusion | bytes 8388864 | tf_op jit(solution)/shard_map/gather | solution.py:201
  34.0 10.3 %all-to-all-start.3 = ((bf16[64,1,64]{2,1,0:T(2,128)(2,1)}), bf16[64,1,64]{2,1,0:T(2,128)(2,1)S(1)}, u32[]{:S(2)}, u32[]{:S(2)}) async-start(bf16[64,1,64]{2,1,0:T(2,128)(2,1)} %copy.234), calls=%async_computation.3 | async-start | bytes 65536 | tf_op jit(solution)/shard_map/all_to_all | solution.py:220
  44.4 8.8 %bitcast_select_fusion = (bf16[64,1,64,4,128]{4,3,2,1,0:T(4,128)(2,1)}, bf16[64,1,64,4,128]{4,3,2,1,0:T(4,128)(2,1)}) fusion(bf16[64,64,4,128]{3,2,1,0:T(4,128)(2,1)} %gather_fusion.4, pred[64]{0:T(512)(128)(4,1)S(1)} %fusion.43, bf16[64,64,4,128]{3,2,1,0:T(4,128)(2,1)} %gather_fusion.2), kind=kLoop, calls=%fused_computation.20 | loop fusion | flops 4194304 | bytes 16777280 | tf_op jit(solution)/shard_map/jit(_where)/select_n | solution.py:202
  53.7 104.5 %all_to_all.32 = bf16[64,1,64,4,128]{4,3,2,1,0:T(4,128)(2,1)} all-to-all(bf16[64,1,64,4,128]{4,3,2,1,0:T(4,128)(2,1)} %get-tuple-element.35), channel_id=1, replica_groups=mesh['batch'=2,'ctx_0'=8,'ctx_1'=4,'ctx_2'=2,'head'=2] {'ctx_0','ctx_1',..., dimensions={0} | all-to-all | bytes 8388608 | tf_op jit(solution)/shard_map/all_to_all | solution.py:206
  158.2 7.6 %all-to-all-start.2 = ((bf16[64,1,64,4,128]{4,3,2,1,0:T(4,128)(2,1)}), bf16[64,1,64,4,128]{4,3,2,1,0:T(4,128)(2,1)}, u32[]{:S(2)}, u32[]{:S(2)}) async-start(bf16[64,1,64,4,128]{4,3,2,1,0:T(4,128)(2,1)} %get-tuple-element.34), calls=%async_computation.2 | async-start | bytes 8388608 | tf_op jit(solution)/shard_map/all_to_all | solution.py:213
  169.1 8.5 %copy.230 = f32[32,4,64,64]{0,1,3,2:T(4,128)} copy(f32[32,4,64,64]{3,2,1,0:T(8,128)} %fusion.7) | data formatting | bytes 4194304 | tf_op jit(solution)/shard_map/bigd,bjgd->bgij/dot_general | solution.py:173
  177.6 4.1 %gather_fusion = f32[64,32,4]{1,2,0:T(4,128)S(1)} fusion(f32[32,4,64,64]{0,1,3,2:T(4,128)} %copy.230, s32[64]{0:T(128)S(1)} %or_bitcast_fusion), kind=kCustom, calls=%fused_computation | custom fusion | bytes 66048 | tf_op jit(solution)/shard_map/jit(diagonal)/gather | solution.py:176
  184.1 8.3 %fusion = f32[4,32,1,64]{3,2,1,0:T(1,128)S(1)} fusion(f32[32,4,64,1]{2,3,0,1:T(1,128)S(1)} %bitcast.411, f32[32,4,64,64]{3,2,1,0:T(8,128)} %fusion.7), kind=kOutput, calls=%fused_computation.22 | convolution fusion | flops 6291456 | bytes 2162688 | tf_op jit(solution)/shard_map/bgij,bgj->bgi/dot_general | solution.py:179
  192.5 4.0 fusion.105
  197.4 3.6 fusion.22
  201.0 3.9 select_reduce_fusion
  207.1 4.2 %gather_fusion.3 = bf16[26,64,4,128]{3,2,1,0:T(4,128)(2,1)S(1)} fusion(bf16[64,64,4,128]{3,2,1,0:T(4,128)(2,1)} %bitcast.401, s32[1024]{0:T(1024)S(1)} %pad_clamp_fusion), kind=kCustom, calls=%fused_computation.3 | custom fusion | bytes 3407976 | tf_op jit(solution)/shard_map/gather | solution.py:240
  212.1 48.4 %all-to-all-done.2 = bf16[64,1,64,4,128]{4,3,2,1,0:T(4,128)(2,1)} async-done(((bf16[64,1,64,4,128]{4,3,2,1,0:T(4,128)(2,1)}), bf16[64,1,64,4,128]{4,3,2,1,0:T(4,128)(2,1)}, u32[]{:S(2)}, u32[]{:S(2)}) %all-to-all-start.2) | async-done | bytes 4194336 | tf_op jit(solution)/shard_map/all_to_all | solution.py:213
  261.3 6.8 %all-to-all-start.4 = ((f32[64,4,4,5]{3,2,1,0:T(4,128)}), f32[64,4,4,5]{3,2,1,0:T(4,128)S(1)}, u32[]{:S(2)}, u32[]{:S(2)}) async-start(f32[64,4,4,5]{3,2,1,0:T(4,128)} %broadcast_in_dim.182), calls=%async_computation.4 | async-start | bytes 1048576 | tf_op jit(solution)/shard_map/all_to_all | solution.py:21
  268.1 5.4 %gather_fusion.5 = bf16[26,64,4,128]{3,2,1,0:T(4,128)(2,1)} fusion(bf16[64,64,4,128]{3,2,1,0:T(4,128)(2,1)} %bitcast.67, s32[1024]{0:T(1024)S(1)} %pad_clamp_fusion), kind=kCustom, calls=%fused_computation.5 | custom fusion | bytes 3407976 | tf_op jit(solution)/shard_map/gather | solution.py:241
  273.5 12.3 %all-to-all-done.4 = f32[64,4,4,5]{3,2,1,0:T(4,128)S(1)} async-done(((f32[64,4,4,5]{3,2,1,0:T(4,128)}), f32[64,4,4,5]{3,2,1,0:T(4,128)S(1)}, u32[]{:S(2)}, u32[]{:S(2)}) %all-to-all-start.4) | async-done | bytes 20512 | tf_op jit(solution)/shard_map/all_to_all | solution.py:21
  291.3 5.9 %all-to-all-start.5 = ((f32[64,1,10320]{2,1,0:T(1,128)}), f32[64,1,10320]{2,1,0:T(1,128)}, u32[]{:S(2)}, u32[]{:S(2)}) async-start(f32[64,1,10320]{2,1,0:T(1,128)} %broadcast_in_dim.184), calls=%async_computation.5 | async-start | bytes 5308416 | tf_op jit(solution)/shard_map/all_to_all | solution.py:21
  297.6 7.8 %fusion.5 = (f32[640]{0:T(1024)S(1)}, f32[640]{0:T(1024)S(1)}, f32[640]{0:T(1024)S(1)}, f32[640]{0:T(1024)S(1)}, f32[640,2048]{1,0:T(8,128)S(1)}) fusion(f32[640,2048]{1,0:T(8,128)} %get-tuple-element.36, f32[640]{0:T(1024)S(1)} %get-tuple-element.18, pred[2048]{0:T(1024)(128)(4,1)S(1)} %add_compare_fusion.1, f32[640]{0:T(1024)S(1)} %get-tuple-element.19, ...), kind=kOutput, calls=%fused_computation.27 | convolution fusion | flops 353891840 | bytes 21677056 | tf_op jit(solution)/shard_map/wrd,td->wrt/dot_general | solution.py:146
  308.1 62.3 %all-gather = f32[64,640]{1,0:T(8,128)S(1)} all-gather(f32[8,640]{1,0:T(8,128)S(1)} %concatenate.17), channel_id=2, replica_groups=mesh['batch'=2,'ctx_0'=8,'ctx_1'=4,'ctx_2'=2,'head'=2] {'ctx_0'}, dimensions={0}, use_global_device_ids=true | all-gather | bytes 184320 | tf_op jit(solution)/shard_map/all_gather | solution.py:50
  370.5 9.2 %all-gather.1 = f32[32,640]{1,0:T(8,128)S(1)} all-gather(f32[8,640]{1,0:T(8,128)S(1)} %pad_maximum_fusion.1), channel_id=3, replica_groups=mesh['batch'=2,'ctx_0'=8,'ctx_1'=4,'ctx_2'=2,'head'=2] {'ctx_1'}, dimensions={0}, use_global_device_ids=true | all-gather | bytes 102400 | tf_op jit(solution)/shard_map/all_gather | solution.py:50
  379.8 10.0 %all-gather.2 = f32[16,640]{1,0:T(8,128)S(1)} all-gather(f32[8,640]{1,0:T(8,128)S(1)} %pad_maximum_fusion.2), channel_id=4, replica_groups=mesh['batch'=2,'ctx_0'=8,'ctx_1'=4,'ctx_2'=2,'head'=2] {'ctx_2'}, dimensions={0}, use_global_device_ids=true | all-gather | bytes 61440 | tf_op jit(solution)/shard_map/all_gather | solution.py:50
  389.9 10.3 %multiply_reduce_fusion.3 = (f32[2048]{0:T(1024)S(1)}, f32[2048]{0:T(1024)S(1)}, f32[2048]{0:T(1024)S(1)}, f32[2048]{0:T(1024)S(1)}) fusion(f32[640,2048]{1,0:T(8,128)} %copy-done.3, f32[640]{0:T(1024)S(1)} %get-tuple-element.4, f32[640]{0:T(1024)S(1)} %get-tuple-element.19, pred[2048]{0:T(1024)(128)(4,1)S(1)} %add_compare_fusion.1, ...), kind=kLoop, calls=%fused_computation.11 | loop fusion | flops 26206208 | bytes 21026816 | tf_op jit(solution)/shard_map/reduce_sum | solution.py:165
  (114 shorter events, 30.0 us)
Async XLA Ops:
  0.6 18.6 %copy-start = (bf16[2048,4,128]{2,1,0:T(4,128)(2,1)S(1)}, bf16[2048,4,128]{2,1,0:T(4,128)(2,1)}, u32[]{:S(2)}) copy-start(bf16[2048,4,128]{2,1,0:T(4,128)(2,1)} %param.10) | copy-start | bytes 6291460
  3.1 30.9 %all-to-all-start.1 = ((bf16[64,1,1]{2,1,0:T(2,128)(2,1)}), bf16[64,1,1]{2,1,0:T(2,128)(2,1)S(1)}, u32[]{:S(2)}, u32[]{:S(2)}) async-start(bf16[64,1,1]{2,1,0:T(2,128)(2,1)} %copy.232), calls=%async_computation.1 | async-start | bytes 65536 | tf_op jit(solution)/shard_map/all_to_all | solution.py:227
  34.0 19.6 %all-to-all-start.3 = ((bf16[64,1,64]{2,1,0:T(2,128)(2,1)}), bf16[64,1,64]{2,1,0:T(2,128)(2,1)S(1)}, u32[]{:S(2)}, u32[]{:S(2)}) async-start(bf16[64,1,64]{2,1,0:T(2,128)(2,1)} %copy.234), calls=%async_computation.3 | async-start | bytes 65536 | tf_op jit(solution)/shard_map/all_to_all | solution.py:220
  158.2 7.7 %copy-start.2 = (bf16[2048,4,128]{2,1,0:T(4,128)(2,1)S(1)}, bf16[2048,4,128]{2,1,0:T(4,128)(2,1)}, u32[]{:S(2)}) copy-start(bf16[2048,4,128]{2,1,0:T(4,128)(2,1)} %param.9) | copy-start | bytes 6291460
  158.2 102.3 %all-to-all-start.2 = ((bf16[64,1,64,4,128]{4,3,2,1,0:T(4,128)(2,1)}), bf16[64,1,64,4,128]{4,3,2,1,0:T(4,128)(2,1)}, u32[]{:S(2)}, u32[]{:S(2)}) async-start(bf16[64,1,64,4,128]{4,3,2,1,0:T(4,128)(2,1)} %get-tuple-element.34), calls=%async_computation.2 | async-start | bytes 8388608 | tf_op jit(solution)/shard_map/all_to_all | solution.py:213
  169.1 14.7 %copy-start.7 = (bf16[4,20,128]{2,0,1:T(4,128)(2,1)S(1)}, bf16[4,20,128]{2,0,1:T(4,128)(2,1)}, u32[]{:S(2)}) copy-start(bf16[4,20,128]{2,0,1:T(4,128)(2,1)} %param.12) | copy-start | bytes 61444
  169.1 14.7 %copy-start.8 = (bf16[4,4,128]{2,1,0:T(4,128)(2,1)S(1)}, bf16[4,4,128]{2,1,0:T(4,128)(2,1)}, u32[]{:S(2)}) copy-start(bf16[4,4,128]{2,1,0:T(4,128)(2,1)} %param.13) | copy-start | bytes 12292
  197.3 7.5 %copy-start.3 = (f32[640,2048]{1,0:T(8,128)}, f32[640,2048]{1,0:T(8,128)S(1)}, u32[]{:S(2)}) copy-start(f32[640,2048]{1,0:T(8,128)S(1)} %fusion.24) | copy-start | bytes 15728644
  211.3 50.0 %copy-start.5 = (bf16[26,64,4,128]{3,2,1,0:T(4,128)(2,1)}, bf16[26,64,4,128]{3,2,1,0:T(4,128)(2,1)S(1)}, u32[]{:S(2)}) copy-start(bf16[26,64,4,128]{3,2,1,0:T(4,128)(2,1)S(1)} %gather_fusion.3) | copy-start | bytes 5111812
  261.3 24.5 %all-to-all-start.4 = ((f32[64,4,4,5]{3,2,1,0:T(4,128)}), f32[64,4,4,5]{3,2,1,0:T(4,128)S(1)}, u32[]{:S(2)}, u32[]{:S(2)}) async-start(f32[64,4,4,5]{3,2,1,0:T(4,128)} %broadcast_in_dim.182), calls=%async_computation.4 | async-start | bytes 1048576 | tf_op jit(solution)/shard_map/all_to_all | solution.py:21
  288.4 9.3 %copy-start.6 = (bf16[2048,1,128]{2,1,0:T(2,128)(2,1)S(1)}, bf16[2048,1,128]{2,1,0:T(2,128)(2,1)}, u32[]{:S(2)}) copy-start(bf16[2048,1,128]{2,1,0:T(2,128)(2,1)} %get-tuple-element.25) | copy-start | bytes 1572868
  291.3 109.6 %all-to-all-start.5 = ((f32[64,1,10320]{2,1,0:T(1,128)}), f32[64,1,10320]{2,1,0:T(1,128)}, u32[]{:S(2)}, u32[]{:S(2)}) async-start(f32[64,1,10320]{2,1,0:T(1,128)} %broadcast_in_dim.184), calls=%async_computation.5 | async-start | bytes 5308416 | tf_op jit(solution)/shard_map/all_to_all | solution.py:21
  297.4 8.1 %slice-start = ((s8[5242880]{0:T(1024)(128)(4,1)}), s8[1048576]{0:T(1024)(128)(4,1)S(1)}, s32[]{:S(2)}) async-start(s8[5242880]{0:T(1024)(128)(4,1)} %bitcast.399), calls=%async_computation.6 | async-start | bytes 2097152
  297.6 7.9 %slice-start.1 = ((s8[5242880]{0:T(1024)(128)(4,1)}), s8[4194304]{0:T(1024)(128)(4,1)S(1)}, s32[]{:S(2)}) async-start(s8[5242880]{0:T(1024)(128)(4,1)} %bitcast.399), calls=%async_computation.7 | async-start | bytes 8388608
  305.4 2.6 copy-start.4
  389.8 14.5 %copy-start.9 = (bf16[4,4,128]{2,1,0:T(4,128)(2,1)S(1)}, bf16[4,4,128]{2,1,0:T(4,128)(2,1)}, u32[]{:S(2)}) copy-start(bf16[4,4,128]{2,1,0:T(4,128)(2,1)} %param.14) | copy-start | bytes 12292
  389.8 15.4 %copy-start.1 = (bf16[2048,4,128]{2,1,0:T(4,128)(2,1)S(1)}, bf16[2048,4,128]{2,1,0:T(4,128)(2,1)}, u32[]{:S(2)}) copy-start(bf16[2048,4,128]{2,1,0:T(4,128)(2,1)} %param.10) | copy-start | bytes 6291460
where the time goes:
time: 414 us; the launch traced here: 406 us
  blocking collectives  186 us (45%)
  waiting for transfers between devices  61.2 us (15%)
  local copies, waits for them, and re-layouts  51.5 us (12%)
  starting transfers between devices  43.7 us (11%)
  matrix products  30.9 us (7%)
  other arithmetic  30.1 us (7%)
    all_to_all x1, blocking collectives, shards(): lax.all_to_all(send_keys.reshape(ctx_count, capacity, BLOCK_TOKENS, head_...  105 us
    all_gather x3, blocking collectives, gathered_once(): both, at, found = (lax.all_gather(jnp.concatenate(lines), axis), 0, {})  81.5 us
    all_to_all x1, waiting for transfers between devices, shards(): lax.all_to_all(send_values.reshape(ctx_count, capacity, BLOCK_TOKENS, hea...  48.4 us
    dot_general x4, matrix products, shards(): jnp.einsum('wrd,td->wrt', grouped[:, head_index], stored_keys[:, head_ind...  16.1 us
    all_to_all x1, starting transfers between devices, shards(): lax.all_to_all(send_used.reshape(ctx_count, capacity), CTX, split_axis=0,...  13.1 us
    all_to_all x2, starting transfers between devices, copy_for_each(): lax.all_to_all(jnp.broadcast_to(value[None], (length, *value.shape)), axi...  12.6 us
    all_to_all x2, waiting for transfers between devices, copy_for_each(): lax.all_to_all(jnp.broadcast_to(value[None], (length, *value.shape)), axi...  12.3 us
    all_to_all x1, starting transfers between devices, shards(): lax.all_to_all(send_live.reshape(ctx_count, capacity, BLOCK_TOKENS), CTX,...  10.3 us
  transfers between devices with their start and end apart: 5, of which 3 were waited for; matrix products, arithmetic and copies ran while one was open for 24% of the time, Pallas kernels for 0%

commit v1 on v0

--- a/solution.py
+++ b/solution.py
@@ -71,48 +71,6 @@
         later_pair[0] - joint_max
     )
     return (joint_max, joint_sum)
-
-
-def decode_partial(
-    queries, block_keys, block_values, block_live, new_keys, new_values, logit_scale
-):
-    step_count = queries.shape[0]
-    cache_logits = (
-        jnp.einsum("sgrd,ngd->sgrn", queries, block_keys, preferred_element_type=jnp.float32)
-        * logit_scale
-    )
-    new_logits = (
-        jnp.einsum("sgrd,ugd->sgru", queries, new_keys, preferred_element_type=jnp.float32)
-        * logit_scale
-    )
-    causal = (
-        jnp.arange(step_count, dtype=jnp.int32)[:, None]
-        >= jnp.arange(step_count, dtype=jnp.int32)[None, :]
-    )
-    causal_bcast = causal[:, None, None, :]
-    live_bcast = block_live[None, None, None, :]
-    local_top = jnp.maximum(
-        jnp.max(jnp.where(live_bcast, cache_logits, MASK_FILL), axis=3),
-        jnp.max(jnp.where(causal_bcast, new_logits, MASK_FILL), axis=3),
-    )
-    row_max = over_copies(local_top, CTX)
-    cache_exp = jnp.where(live_bcast, jnp.exp(cache_logits - row_max[..., None]), 0.0)
-    cache_weighted = jnp.einsum(
-        "sgrn,ngd->sgrd",
-        cache_exp.astype(jnp.bfloat16),
-        block_values,
-        preferred_element_type=jnp.float32,
-    )
-    weighted, denominator = in_one((cache_weighted, jnp.sum(cache_exp, axis=3)), CTX)
-    new_exp = jnp.where(causal_bcast, jnp.exp(new_logits - row_max[..., None]), 0.0)
-    weighted = weighted + jnp.einsum(
-        "sgru,ugd->sgrd",
-        new_exp.astype(jnp.bfloat16),
-        new_values,
-        preferred_element_type=jnp.float32,
-    )
-    denominator = denominator + jnp.sum(new_exp, axis=3)
-    return weighted / denominator[..., None]
 
 
 def shards(
@@ -150,6 +108,28 @@
             preferred_element_type=jnp.float32,
         )
         logit_list.append(product.reshape(window_rows * group_size, tokens) * logit_scale)
+    keep_row = keep_lists[0]
+    owner_row = owner_ids[0]
+    kept_here = jnp.any(
+        keep_row[None, :] == jnp.arange(blocks_here, dtype=jnp.int32)[:, None], axis=1
+    )
+    kept_live = jnp.repeat(kept_here, BLOCK_TOKENS) & is_live
+    kept_mask = kept_live[None, None, None, :]
+    step_rows = decoded_queries.reshape(step_count, head_count, group_size, head_width)
+    cache_logits = (
+        jnp.einsum("sgrd,ngd->sgrn", step_rows, stored_keys, preferred_element_type=jnp.float32)
+        * logit_scale
+    )
+    new_logits = (
+        jnp.einsum("sgrd,ugd->sgru", step_rows, step_keys, preferred_element_type=jnp.float32)
+        * logit_scale
+    )
+    steps = jnp.arange(step_count, dtype=jnp.int32)
+    causal = (steps[:, None] >= steps[None, :])[:, None, None, :]
+    step_top = jnp.maximum(
+        jnp.max(jnp.where(kept_mask, cache_logits, MASK_FILL), axis=3),
+        jnp.max(jnp.where(causal, new_logits, MASK_FILL), axis=3),
+    )
     local_max = jnp.stack(
         [jnp.max(jnp.where(live_mask, logit_rows, MASK_FILL), axis=1) for logit_rows in logit_list]
     )
@@ -158,7 +138,41 @@
         for head_index in range(head_count)
     ]
     local_sum = jnp.stack([jnp.sum(exp_rows, axis=1) for exp_rows in exp_list])
-    row_max, row_sum = combined_by_axis((local_max, local_sum), CTX, merge_stats)
+    row_max, row_sum = (local_max, local_sum)
+    step_max = step_top
+    for axis in (("ctx_1", "ctx_2"), ("ctx_0",)):
+        both = lax.all_gather(
+            jnp.concatenate([row_max.ravel(), row_sum.ravel(), step_max.ravel()]), axis
+        )
+        cut = row_max.size
+        every_max = both[:, :cut]
+        joint = jnp.max(every_max, axis=0)
+        row_sum = jnp.sum(both[:, cut : 2 * cut] * jnp.exp(every_max - joint), axis=0).reshape(
+            row_max.shape
+        )
+        row_max = joint.reshape(row_max.shape)
+        step_max = jnp.max(both[:, 2 * cut :], axis=0).reshape(step_max.shape)
+    cache_exp = jnp.where(kept_mask, jnp.exp(cache_logits - step_max[..., None]), 0.0)
+    cache_weighted = jnp.einsum(
+        "sgrn,ngd->sgrd",
+        cache_exp.astype(jnp.bfloat16),
+        stored_values,
+        preferred_element_type=jnp.float32,
+    )
+    weighted = jnp.concatenate([cache_weighted.ravel(), jnp.sum(cache_exp, axis=3).ravel()])
+    for axis in (("ctx_1", "ctx_2"), ("ctx_0",)):
+        weighted = jnp.sum(lax.all_gather(weighted, axis), axis=0)
+    denominator = weighted[cache_weighted.size :].reshape(step_max.shape)
+    weighted = weighted[: cache_weighted.size].reshape(cache_weighted.shape)
+    new_exp = jnp.where(causal, jnp.exp(new_logits - step_max[..., None]), 0.0)
+    weighted = weighted + jnp.einsum(
+        "sgru,ugd->sgrd",
+        new_exp.astype(jnp.bfloat16),
+        decoded_values,
+        preferred_element_type=jnp.float32,
+    )
+    denominator = denominator + jnp.sum(new_exp, axis=3)
+    attended = weighted / denominator[..., None]
     rescale = jnp.exp(local_max - row_max) / row_sum
     weight_sum = jnp.stack(
         [
@@ -184,8 +198,6 @@
     token_scores = jnp.where(
         live_mask, LAMBDA * importance - (1.0 - LAMBDA) * redundancy_score, 0.0
     )
-    keep_row = keep_lists[0]
-    owner_row = owner_ids[0]
     capacity = (kept_count + ctx_count - 1) // ctx_count
     slot_total = ctx_count * capacity
     kept_range = jnp.arange(kept_count, dtype=jnp.int32)
@@ -200,9 +212,8 @@
     used_mask = slot_used[:, None, None, None]
     send_keys = jnp.where(used_mask, blocked_keys[slot_block], jnp.zeros((), jnp.bfloat16))
     send_values = jnp.where(used_mask, value_blocks[slot_block], jnp.zeros((), jnp.bfloat16))
-    send_live = jnp.where(slot_used[:, None], live_blocks[slot_block], 0.0).astype(jnp.bfloat16)
     send_used = slot_used.astype(jnp.bfloat16)
-    got_keys, got_values, got_live, got_used = (
+    got_keys, got_values, got_used = (
         lax.all_to_all(
             send_keys.reshape(ctx_count, capacity, BLOCK_TOKENS, head_count, head_width),
             CTX,
@@ -218,19 +229,11 @@
             tiled=True,
         ),
         lax.all_to_all(
-            send_live.reshape(ctx_count, capacity, BLOCK_TOKENS),
-            CTX,
-            split_axis=0,
-            concat_axis=0,
-            tiled=True,
-        ),
-        lax.all_to_all(
             send_used.reshape(ctx_count, capacity), CTX, split_axis=0, concat_axis=0, tiled=True
         ),
     )
     recv_keys = got_keys.reshape(slot_total, BLOCK_TOKENS, head_count, head_width)
     recv_values = got_values.reshape(slot_total, BLOCK_TOKENS, head_count, head_width)
-    recv_live = got_live.reshape(slot_total, BLOCK_TOKENS)
     used_int = (got_used.reshape(slot_total) > 0.5).astype(jnp.int32)
     slot_rank = jnp.cumsum(used_int) - 1
     pick_match = (slot_rank[None, :] == kept_range[:, None]) & (used_int[None, :] > 0)
@@ -239,11 +242,6 @@
     )
     retained_keys = recv_keys[picked].reshape(kept_count * BLOCK_TOKENS, head_count, head_width)
     retained_values = recv_values[picked].reshape(kept_count * BLOCK_TOKENS, head_count, head_width)
-    kept_live = recv_live[picked].reshape(kept_count * BLOCK_TOKENS) > 0.5
-    step_rows = decoded_queries.reshape(step_count, head_count, group_size, head_width)
-    attended = decode_partial(
-        step_rows, retained_keys, retained_values, kept_live, step_keys, decoded_values, logit_scale
-    )
     decoded = attended.reshape(step_count, head_count * group_size, head_width).astype(jnp.bfloat16)
     return (token_scores, retained_keys, retained_values, decoded)
 

time: 414 us -> 481 us (1.16)
  waiting for transfers between devices: 61.2 us -> 306 us
  blocking collectives: 186 us -> 0 us
  between operations: 2.34 us -> 17.6 us
  local copies, waits for them, and re-layouts: 51.5 us -> 63.9 us
  starting transfers between devices: 43.7 us -> 31.4 us
  matrix products: 30.9 us -> 25.1 us
    unnamed x0 -> x8, waiting for transfers between devices: none -> 233 us
    all_to_all x1 -> x0, blocking collectives: 105 us -> none  [shards(): lax.all_to_all(send_keys.reshape(ctx_count, capacity, BLOCK_TOKENS, head_...]
    all_gather x3 -> x0, blocking collectives: 81.5 us -> none  [gathered_once(): both, at, found = (lax.all_gather(jnp.concatenate(lines), axis), 0, {})]
    all_to_all x3 -> x1, waiting for transfers between devices: 12.8 us -> 72.7 us  [shards(): lax.all_to_all(send_keys.reshape(ctx_count, capacity, BLOCK_TOKENS, head_...]
    all_to_all x1, waiting for transfers between devices: 48.4 us -> 0.01 us  [shards(): lax.all_to_all(send_values.reshape(ctx_count, capacity, BLOCK_TOKENS, hea...]
    all_to_all x3 -> x1, starting transfers between devices: 22.9 us -> 10.5 us  [shards(): lax.all_to_all(send_keys.reshape(ctx_count, capacity, BLOCK_TOKENS, head_...]
    dot_general x4, matrix products: 16.1 us -> 7.74 us  [shards(): jnp.einsum('wrd,td->wrt', grouped[:, head_index], stored_keys[:, head_ind...]
    unnamed x29 -> x39, local copies, waits for them, and re-layouts: 0.56 us -> 8.9 us
  transfers between devices with their start and end apart: 5 -> 7, of which waited for: 3 -> 5; matrix products, arithmetic and copies ran while one was open for 24% -> 22% of each run, Pallas kernels for 0% -> 0%
where the time goes in v1:
time: 481 us; the launch traced here: 476 us
  waiting for transfers between devices  306 us (64%)
  local copies, waits for them, and re-layouts  63.9 us (13%)
  other arithmetic  32.3 us (7%)
  starting transfers between devices  31.4 us (7%)
  matrix products  25.1 us (5%)
  between operations  17.6 us (4%)
    unnamed x8, waiting for transfers between devices  233 us
    all_to_all x1, waiting for transfers between devices, shards(): lax.all_to_all(send_keys.reshape(ctx_count, capacity, BLOCK_TOKENS, head_...  72.7 us
    all_to_all x1, starting transfers between devices, shards(): lax.all_to_all(send_used.reshape(ctx_count, capacity), CTX, split_axis=0,...  13.1 us
    all_to_all x1, starting transfers between devices, shards(): lax.all_to_all(send_keys.reshape(ctx_count, capacity, BLOCK_TOKENS, head_...  10.5 us
    reduce_sum x1, other arithmetic, shards(): jnp.sum(exp_list[head_index] * rescale[head_index][:, None], axis=0)  10.1 us
  transfers between devices with their start and end apart: 7, of which 5 were waited for; matrix products, arithmetic and copies ran while one was open for 22% of the time, Pallas kernels for 0%

profile of v1, /device:TPU:1, one launch (start us, length us, event | category | flops | bytes accessed | tf_op | source)
XLA Modules:
  0.0 475.8 jit_solution(6223415526395403770)
XLA Ops:
  9.7 13.1 %all-to-all-start.1 = ((bf16[64,1,1]{2,1,0:T(2,128)(2,1)}), bf16[64,1,1]{2,1,0:T(2,128)(2,1)S(1)}, u32[]{:S(2)}, u32[]{:S(2)}) async-start(bf16[64,1,1]{2,1,0:T(2,128)(2,1)} %copy.175), calls=%async_computation.1 | async-start | bytes 65536 | tf_op jit(solution)/shard_map/all_to_all | solution.py:231
  24.4 7.9 %gather_fusion.2 = bf16[64,64,4,128]{3,2,1,0:T(4,128)(2,1)} fusion(bf16[32,64,4,128]{3,2,1,0:T(4,128)(2,1)} %bitcast.142, s32[1024]{0:T(1024)S(1)} %pad_clamp_fusion.1), kind=kCustom, calls=%fused_computation.2 | custom fusion | bytes 8388864 | tf_op jit(solution)/shard_map/gather | solution.py:213
  32.3 6.3 %gather_fusion.4 = bf16[64,64,4,128]{3,2,1,0:T(4,128)(2,1)} fusion(bf16[32,64,4,128]{3,2,1,0:T(4,128)(2,1)S(1)} %bitcast.138, s32[1024]{0:T(1024)S(1)} %pad_clamp_fusion.1), kind=kCustom, calls=%fused_computation.4 | custom fusion | bytes 8388864 | tf_op jit(solution)/shard_map/gather | solution.py:214
  38.6 8.8 %bitcast_select_fusion = (bf16[64,1,64,4,128]{4,3,2,1,0:T(4,128)(2,1)}, bf16[64,1,64,4,128]{4,3,2,1,0:T(4,128)(2,1)}) fusion(bf16[64,64,4,128]{3,2,1,0:T(4,128)(2,1)} %gather_fusion.4, pred[64]{0:T(512)(128)(4,1)S(1)} %fusion.44, bf16[64,64,4,128]{3,2,1,0:T(4,128)(2,1)} %gather_fusion.2), kind=kLoop, calls=%fused_computation.18 | loop fusion | flops 4194304 | bytes 16777280 | tf_op jit(solution)/shard_map/jit(_where)/select_n | solution.py:214
  47.4 10.5 %all-to-all-start = ((bf16[64,1,64,4,128]{4,3,2,1,0:T(4,128)(2,1)}), bf16[64,1,64,4,128]{4,3,2,1,0:T(4,128)(2,1)}, u32[]{:S(2)}, u32[]{:S(2)}) async-start(bf16[64,1,64,4,128]{4,3,2,1,0:T(4,128)(2,1)} %get-tuple-element.30), calls=%async_computation | async-start | bytes 8388608 | tf_op jit(solution)/shard_map/all_to_all | solution.py:217
  60.6 7.8 %fusion.60 = (bf16[2048,1,128]{2,1,0:T(2,128)(2,1)S(1)}, bf16[2048,1,128]{2,1,0:T(2,128)(2,1)S(1)}, bf16[2048,1,128]{2,1,0:T(2,128)(2,1)S(1)}, bf16[2048,1,128]{2,1,0:T(2,128)(2,1)S(1)}) fusion(bf16[2048,4,128]{2,1,0:T(4,128)(2,1)} %param.9), kind=kLoop, calls=%fused_computation.135 | loop fusion | bytes 4194304 | tf_op jit(solution)/shard_map/slice | solution.py:107
  71.5 1.7 copy-done.3
  73.3 1.5 copy-done.4
  74.8 5.1 %fusion.2 = (f32[640]{0:T(1024)S(1)}, f32[640]{0:T(1024)S(1)}, f32[640]{0:T(1024)S(1)}, f32[640]{0:T(1024)S(1)}, f32[640,2048]{1,0:T(8,128)}) fusion(f32[640,2048]{1,0:T(8,128)S(1)} %get-tuple-element.36, f32[640]{0:T(1024)S(1)} %get-tuple-element.35, pred[2048]{0:T(1024)(128)(4,1)S(1)} %add_compare_fusion.1, f32[640,2048]{1,0:T(8,128)S(1)} %fusion.23, ...), kind=kOutput, calls=%fused_computation.22 | convolution fusion | flops 352581120 | bytes 21674496 | tf_op jit(solution)/shard_map/wrd,td->wrt/dot_general | solution.py:104
  79.9 72.7 %all-to-all-done = bf16[64,1,64,4,128]{4,3,2,1,0:T(4,128)(2,1)} async-done(((bf16[64,1,64,4,128]{4,3,2,1,0:T(4,128)(2,1)}), bf16[64,1,64,4,128]{4,3,2,1,0:T(4,128)(2,1)}, u32[]{:S(2)}, u32[]{:S(2)}) %all-to-all-start) | async-done | bytes 4194336 | tf_op jit(solution)/shard_map/all_to_all | solution.py:217
  152.6 7.1 %all-to-all-start.2 = ((bf16[64,1,64,4,128]{4,3,2,1,0:T(4,128)(2,1)}), bf16[64,1,64,4,128]{4,3,2,1,0:T(4,128)(2,1)}, u32[]{:S(2)}, u32[]{:S(2)}) async-start(bf16[64,1,64,4,128]{4,3,2,1,0:T(4,128)(2,1)} %get-tuple-element.29), calls=%async_computation.2 | async-start | bytes 8388608 | tf_op jit(solution)/shard_map/all_to_all | solution.py:224
  159.8 7.3 %fusion.3 = (f32[640]{0:T(1024)S(1)}, f32[640]{0:T(1024)S(1)}, f32[640]{0:T(1024)S(1)}) fusion(f32[640,2048]{1,0:T(8,128)} %get-tuple-element.37, f32[640]{0:T(1024)S(1)} %get-tuple-element.13, pred[2048]{0:T(1024)(128)(4,1)S(1)} %add_compare_fusion.1, f32[640]{0:T(1024)S(1)} %get-tuple-element.14, f32[640,2048]{1,0:T(8,128)} %copy-done.3, ...), kind=kLoop, calls=%fused_computation.23 | loop fusion | flops 15726720 | bytes 15746048 | tf_op jit(solution)/shard_map/reduce_sum | solution.py:140
  167.9 2.5 select_reduce_fusion.4
  175.3 5.4 %fusion.10 = f32[32,4,64,64]{3,2,1,0:T(8,128)} fusion(bf16[32,64,4,128]{3,2,1,0:T(4,128)(2,1)} %bitcast.144), kind=kOutput, calls=%fused_computation.31 | convolution fusion | flops 134217728 | bytes 4194304 | tf_op jit(solution)/shard_map/bigd,bjgd->bgij/dot_general | solution.py:187
  180.7 8.5 %copy.173 = f32[32,4,64,64]{0,1,3,2:T(4,128)} copy(f32[32,4,64,64]{3,2,1,0:T(8,128)} %fusion.10) | data formatting | bytes 4194304 | tf_op jit(solution)/shard_map/bigd,bjgd->bgij/dot_general | solution.py:187
  189.2 4.2 gather_fusion
  193.6 8.3 %fusion = f32[4,32,1,64]{3,2,1,0:T(1,128)S(1)} fusion(f32[32,4,64,1]{2,3,0,1:T(1,128)S(1)} %bitcast.149, f32[32,4,64,64]{3,2,1,0:T(8,128)} %fusion.10), kind=kOutput, calls=%fused_computation.20 | convolution fusion | flops 6291456 | bytes 2162688 | tf_op jit(solution)/shard_map/bgij,bgj->bgi/dot_general | solution.py:193
  203.7 38.1 %all-reduce.9.cloned.1.call-done = f32[41600]{0:T(1024)} async-done(((f32[41600]{0:T(1024)}), f32[41600]{0:T(1024)}) %all-reduce.9.cloned.1.call-update) | async-done | bytes 166416
  244.0 70.9 %all-reduce.11.cloned.1.call-done = f32[41600]{0:T(1024)} async-done(((f32[41600]{0:T(1024)}), f32[41600]{0:T(1024)}) %all-reduce.11.cloned.1.call-update) | async-done | bytes 166416
  318.7 10.1 %multiply_reduce_fusion.3 = (f32[2048]{0:T(1024)S(1)}, f32[2048]{0:T(1024)S(1)}, f32[2048]{0:T(1024)S(1)}, f32[2048]{0:T(1024)S(1)}) fusion(f32[640,2048]{1,0:T(8,128)} %copy-done.4, f32[640]{0:T(1024)S(1)} %get-tuple-element.4, f32[640]{0:T(1024)S(1)} %get-tuple-element.35, pred[2048]{0:T(1024)(128)(4,1)S(1)} %add_compare_fusion.1, ...), kind=kLoop, calls=%fused_computation.9 | loop fusion | flops 26206208 | bytes 21026816 | tf_op jit(solution)/shard_map/reduce_sum | solution.py:179
  329.0 55.7 %all-reduce.13.cloned.1.call-done = f32[82560]{0:T(1024)} async-done(((f32[82560]{0:T(1024)}), f32[82560]{0:T(1024)}) %all-reduce.13.cloned.1.call-update) | async-done | bytes 330256
  388.1 68.1 %all-reduce.15.cloned.1.call-done = f32[82560]{0:T(1024)} async-done(((f32[82560]{0:T(1024)}), f32[82560]{0:T(1024)}) %all-reduce.15.cloned.1.call-update) | async-done | bytes 330256
  458.5 5.4 %gather_fusion.3 = bf16[26,64,4,128]{3,2,1,0:T(4,128)(2,1)} fusion(bf16[64,64,4,128]{3,2,1,0:T(4,128)(2,1)} %bitcast.35, s32[1024]{0:T(1024)S(1)} %pad_clamp_fusion), kind=kCustom, calls=%fused_computation.3 | custom fusion | bytes 3407976 | tf_op jit(solution)/shard_map/gather | solution.py:243
  463.9 5.4 %gather_fusion.5 = bf16[26,64,4,128]{3,2,1,0:T(4,128)(2,1)} fusion(bf16[64,64,4,128]{3,2,1,0:T(4,128)(2,1)} %bitcast.43, s32[1024]{0:T(1024)S(1)} %pad_clamp_fusion), kind=kCustom, calls=%fused_computation.5 | custom fusion | bytes 3407976 | tf_op jit(solution)/shard_map/gather | solution.py:244
  (138 shorter events, 25.9 us)
Async XLA Ops:
  7.2 25.1 %copy-start = (bf16[2048,4,128]{2,1,0:T(4,128)(2,1)S(1)}, bf16[2048,4,128]{2,1,0:T(4,128)(2,1)}, u32[]{:S(2)}) copy-start(bf16[2048,4,128]{2,1,0:T(4,128)(2,1)} %param.10) | copy-start | bytes 6291460
  9.7 37.7 %all-to-all-start.1 = ((bf16[64,1,1]{2,1,0:T(2,128)(2,1)}), bf16[64,1,1]{2,1,0:T(2,128)(2,1)S(1)}, u32[]{:S(2)}, u32[]{:S(2)}) async-start(bf16[64,1,1]{2,1,0:T(2,128)(2,1)} %copy.175), calls=%async_computation.1 | async-start | bytes 65536 | tf_op jit(solution)/shard_map/all_to_all | solution.py:231
  47.4 105.2 %all-to-all-start = ((bf16[64,1,64,4,128]{4,3,2,1,0:T(4,128)(2,1)}), bf16[64,1,64,4,128]{4,3,2,1,0:T(4,128)(2,1)}, u32[]{:S(2)}, u32[]{:S(2)}) async-start(bf16[64,1,64,4,128]{4,3,2,1,0:T(4,128)(2,1)} %get-tuple-element.30), calls=%async_computation | async-start | bytes 8388608 | tf_op jit(solution)/shard_map/all_to_all | solution.py:217
  69.2 2.3 copy-start.2
  70.1 3.2 copy-start.3
  71.1 3.7 copy-start.4
  152.6 311.3 %all-to-all-start.2 = ((bf16[64,1,64,4,128]{4,3,2,1,0:T(4,128)(2,1)}), bf16[64,1,64,4,128]{4,3,2,1,0:T(4,128)(2,1)}, u32[]{:S(2)}, u32[]{:S(2)}) async-start(bf16[64,1,64,4,128]{4,3,2,1,0:T(4,128)(2,1)} %get-tuple-element.29), calls=%async_computation.2 | async-start | bytes 8388608 | tf_op jit(solution)/shard_map/all_to_all | solution.py:224
  159.7 82.1 %all-reduce.9.cloned.1.call-start = ((), (), s32[]{:S(2)}) async-start(), calls=%async_computation.3 | async-start | bytes 335872
  159.8 7.6 %copy-start.1 = (s32[1,26]{1,0:T(1,128)S(1)}, s32[1,26]{1,0:T(1,128)}, u32[]{:S(2)}) copy-start(s32[1,26]{1,0:T(1,128)} %param.15) | copy-start | bytes 316
  159.8 7.9 %copy-start.9 = (bf16[4,20,128]{2,0,1:T(4,128)(2,1)S(1)}, bf16[4,20,128]{2,0,1:T(4,128)(2,1)}, u32[]{:S(2)}) copy-start(bf16[4,20,128]{2,0,1:T(4,128)(2,1)} %param.12) | copy-start | bytes 61444
  159.8 7.9 %copy-start.10 = (bf16[4,4,128]{2,1,0:T(4,128)(2,1)S(1)}, bf16[4,4,128]{2,1,0:T(4,128)(2,1)}, u32[]{:S(2)}) copy-start(bf16[4,4,128]{2,1,0:T(4,128)(2,1)} %param.13) | copy-start | bytes 12292
  159.8 10.8 %copy-start.13 = (u32[256]{0:T(256)S(1)}, u32[256]{0:T(256)}, u32[]{:S(2)}) copy-start(u32[256]{0:T(256)} %constant.109) | copy-start | bytes 3076
  159.8 13.1 %copy-start.12 = (u32[256]{0:T(256)S(1)}, u32[256]{0:T(256)}, u32[]{:S(2)}) copy-start(u32[256]{0:T(256)} %constant.114) | copy-start | bytes 3076
  171.9 0.7 copy-start.7
  172.6 142.2 %all-reduce.11.cloned.1.call-start = ((), (), s32[]{:S(2)}) async-start(), calls=%async_computation.4 | async-start | bytes 335872
  243.2 0.7 copy-start.8
  243.9 140.8 %all-reduce.13.cloned.1.call-start = ((), (), s32[]{:S(2)}) async-start(), calls=%async_computation.5 | async-start | bytes 663552
  317.5 0.7 copy-start.5
  318.2 137.9 %all-reduce.15.cloned.1.call-start = ((), (), s32[]{:S(2)}) async-start(), calls=%async_computation.6 | async-start | bytes 663552
  318.7 138.8 %copy-start.11 = (bf16[4,4,128]{2,1,0:T(4,128)(2,1)S(1)}, bf16[4,4,128]{2,1,0:T(4,128)(2,1)}, u32[]{:S(2)}) copy-start(bf16[4,4,128]{2,1,0:T(4,128)(2,1)} %param.14) | copy-start | bytes 12292
  386.6 0.7 copy-start.6
Sparse Core Ops, SparseCore 0:
  172.7 69.0 all-reduce.8
  244.7 70.0 all-reduce.10
  318.4 66.2 all-reduce.12
  387.5 68.5 all-reduce.14

commit v2 on v0

v2 whole, which is shorter than its diff:
```python
import functools
import math

import jax
import jax.numpy as jnp
from jax import lax
from jax.experimental import pallas as pl
from jax.experimental.pallas import tpu as pltpu
from jax.sharding import Mesh
from jax.sharding import PartitionSpec as P

BLOCK = 64
CTX = ("ctx_0", "ctx_1", "ctx_2")
BATCH_CTX = ("batch", "ctx_0", "ctx_1", "ctx_2")
MESH = pl.DeviceIdType.MESH
FAR = -1e30
LAMBDA = 0.1
NORM_EPS = 1e-06
NZ = 8
LANES = 8
HALF = NZ // 2
STEP_ROWS = 80
FITS_ALL = (26, 20, 12, 4)
FITS_MOST = (17, 14, 10, 5)
F32, BF16, I32 = jnp.float32, jnp.bfloat16, jnp.int32


def contract_last(a, b):
    return lax.dot_general(a, b, (((1,), (1,)), ((), ())), preferred_element_type=F32)


def row_to_column(row, rows):
    return jnp.transpose(jnp.broadcast_to(row, (128, 128)))[:rows, :1]


def column_to_row(column):
    rows = column.shape[0]
    wide = jnp.concatenate(
        [jnp.broadcast_to(column, (rows, 128)), jnp.zeros((128 - rows, 128), F32)], axis=0
    )
    return jnp.transpose(wide)[:1, :]


def exchange(
    slots,
    scale2,
    table,
    lists,
    picks,
    local_live,
    keys,
    values,
    queries,
    step_queries,
    new_keys,
    new_values,
    kept_bias,
    head_bias,
    new_bias,
    aux,
    out_scores,
    out_keys,
    out_values,
    out_decoded,
    zs_p,
    zs_m,
    zr_p1,
    zr_p2,
    zr_p3,
    zr_m1,
    zr_m2,
    zr_m3,
    zr_4,
    yb,
    yr,
    kf,
    probs,
    chunk_max,
    chunk_sum,
    redundancy,
    dl,
    rescale,
    stat_plane,
    stat_ring,
    sum_plane,
    sum_ring,
    z_send,
    z_recv,
    y_send,
    y_recv,
    s_send,
    s_recv,
):
    me_z = lax.axis_index("ctx_0")
    me_lane = lax.axis_index("ctx_1") * 2 + lax.axis_index("ctx_2")
    s1, s2, s3, s4 = slots

    def ring_peer(k):
        return {"ctx_0": lax.rem(me_z + (k + NZ), NZ)}

    def plane_peer(i):
        lane = lax.rem(me_lane + i, LANES)
        return {"ctx_1": lane // 2, "ctx_2": lax.rem(lane, 2)}

    barrier = pltpu.get_barrier_semaphore()
    for i in range(1, LANES):
        pl.semaphore_signal(barrier, inc=1, device_id=plane_peer(i), device_id_type=MESH)
    for k in range(1, NZ):
        pl.semaphore_signal(barrier, inc=1, device_id=ring_peer(k), device_id_type=MESH)

    def pack_lists(slot, carry):
        for way, dst in ((0, zs_p), (1, zs_m)):
            at = lists[way, slot]
            dst[slot, 0] = keys[at]
            dst[slot, 1] = values[at]
        return carry

    lax.fori_loop(0, s1, pack_lists, 0)

    def own_slot(i):
        at = table[0, lax.rem(me_lane + i, LANES)]
        return keys[at], values[at]

    for i in range(1, LANES):
        yb[0, i, 0], yb[0, i, 1] = own_slot(i)
    here = me_z * LANES + me_lane
    yr[here, 0], yr[here, 1] = own_slot(0)

    pl.semaphore_wait(barrier, LANES - 1 + NZ - 1)

    segments = ((0, s4), (s4, s3), (s3, s2), (s2, s1))
    ring = (
        (zs_p, zr_p1, zr_p2, zr_p3),
        (zs_m, zr_m1, zr_m2, zr_m3),
    )
    ring_copies = {}

    def ring_start(way, q, hop):
        a, b = segments[q]
        if a == b:
            return
        src = ring[way][hop - 1].at[pl.ds(a, b - a)]
        if hop < HALF:
            dst = ring[way][hop].at[pl.ds(a, b - a)]
        else:
            dst = zr_4.at[pl.ds(way * s4 + a, b - a)]
        number = q * HALF + hop - 1
        copy = pltpu.make_async_remote_copy(
            src_ref=src,
            dst_ref=dst,
            send_sem=z_send.at[way, number],
            recv_sem=z_recv.at[way, number],
            device_id=ring_peer(1 if way == 0 else -1),
            device_id_type=MESH,
        )
        copy.start()
        ring_copies[way, q, hop] = copy

    def ring_arrived(way, q, hop):
        if (way, q, hop) in ring_copies:
            ring_copies[way, q, hop].wait_recv()

    def hand_on(q, hop):
        for way in range(2):
            ring_arrived(way, q, hop)
            ring_start(way, q, hop + 1)

    arrivals = {1: zr_p1, 2: zr_p2, 3: zr_p3, 4: zr_4, 5: zr_m3, 6: zr_m2, 7: zr_m1}
    plane_copies = {}
    order = (0, 1, 7, 2, 6, 3, 5, 4)
    depth = yb.shape[0]

    def plane_pack(b):
        at = order.index(b)
        if at >= depth:
            for i in range(1, LANES):
                plane_copies[order[at - depth], i].wait_send()
        source = lax.rem(me_z + (NZ - b), NZ) * LANES + me_lane
        got = arrivals[b]
        for i in range(LANES):
            slot = table[b, lax.rem(me_lane + i, LANES)]
            if i == 0:
                yr[source] = got[slot]
            else:
                yb[at % depth, i] = got[slot]

    def plane_start(b):
        at = order.index(b)
        source = lax.rem(me_z + (NZ - b), NZ) * LANES + me_lane
        for i in range(1, LANES):
            copy = pltpu.make_async_remote_copy(
                src_ref=yb.at[at % depth, i],
                dst_ref=yr.at[source],
                send_sem=y_send.at[b, i],
                recv_sem=y_recv.at[b, i],
                device_id=plane_peer(i),
                device_id_type=MESH,
            )
            copy.start()
            plane_copies[b, i] = copy

    def share(buffer, number, at, peer, count):
        copies = []
        for i in range(1, count):
            copy = pltpu.make_async_remote_copy(
                src_ref=buffer.at[at],
                dst_ref=buffer.at[at],
                send_sem=s_send.at[number, i],
                recv_sem=s_recv.at[number, i],
                device_id=peer(i),
                device_id_type=MESH,
            )
            copy.start()
            copies.append(copy)
        return copies

    def settle(copies):
        for copy in copies:
            copy.wait()

    for q in range(HALF):
        for way in range(2):
            ring_start(way, q, 1)
    plane_start(0)

    def widen(c, carry):
        kf[pl.ds(pl.multiple_of(c * 256, 256), 256), :] = keys[c].astype(F32)
        return carry

    lax.fori_loop(0, 32, widen, 0)
    live_here = local_live[0]
    rows = lax.broadcasted_iota(I32, (256, 256), 0)
    columns = lax.broadcasted_iota(I32, (256, 256), 1)

    def score(i, carry):
        g, c = i // 8, lax.rem(i, 8)
        chunk = kf[pl.ds(c * 1024 + g, 256, stride=4), :].astype(BF16)
        live = lax.broadcasted_iota(I32, (256, 128), 0) + c * 256 < live_here
        bias = jnp.where(live, 0.0, FAR)
        logits = contract_last(chunk, queries[g]) + jnp.concatenate([bias] * 5, axis=1)
        largest = jnp.max(logits, axis=0, keepdims=True)
        weights = jnp.exp2((logits - largest) * scale2)
        chunk_max[pl.ds(i, 1), :] = largest
        chunk_sum[pl.ds(i, 1), :] = jnp.sum(weights, axis=0, keepdims=True)
        probs[i] = weights.astype(BF16)
        gram = contract_last(chunk, chunk)
        on_diagonal = jnp.where(rows == columns, gram, 0.0)
        across = jnp.sum(on_diagonal, axis=0, keepdims=True)
        down = jnp.sum(on_diagonal, axis=1, keepdims=True)
        spread = jnp.where(live[:, :1], 1.0, 0.0) / jnp.sqrt(down + NORM_EPS)
        norm = jnp.sqrt(across + NORM_EPS)
        together = jnp.where(rows // BLOCK == columns // BLOCK, gram, 0.0)
        row_sum = jnp.sum(together * spread, axis=0, keepdims=True) / norm
        own = aux[pl.ds(c, 1), :] * across / (norm * norm)
        redundancy[pl.ds(i, 1), :] = (row_sum - own) / aux[pl.ds(c + 8, 1), :]
        return carry

    lax.fori_loop(0, 32, score, 0)

    def decode_logits(c, top):
        chunk = keys[pl.ds(c * 4, 4)].reshape(1024, 128)
        found = contract_last(step_queries[...], chunk)
        found = found + jnp.concatenate([head_bias[...]] * 8, axis=1) + kept_bias[pl.ds(c, 1), :]
        dl[c] = found
        for part in range(8):
            top = jnp.maximum(top, found[:, part * 128 : (part + 1) * 128])
        return top

    new_logits = contract_last(step_queries[...], new_keys[...]) + new_bias[...]
    top = lax.fori_loop(0, 8, decode_logits, new_logits)
    step_top = column_to_row(jnp.max(top, axis=1, keepdims=True))

    maxima, sums = [], []
    for g in range(4):
        part_max = chunk_max[g * 8 : g * 8 + 8, :]
        largest = jnp.max(part_max, axis=0, keepdims=True)
        maxima.append(largest)
        sums.append(
            jnp.sum(
                chunk_sum[g * 8 : g * 8 + 8, :] * jnp.exp2((part_max - largest) * scale2),
                axis=0,
                keepdims=True,
            )
        )
    stat_plane[me_lane, :, :640] = jnp.concatenate(maxima + sums, axis=0)
    stat_plane[me_lane, :, 640:] = jnp.broadcast_to(step_top, (8, 128))
    stats = share(stat_plane, 0, me_lane, plane_peer, LANES)
    hand_on(0, 1)

    def merged(buffer, count):
        largest = buffer[0, :4, :640]
        step_max = buffer[0, :, 640:]
        for k in range(1, count):
            largest = jnp.maximum(largest, buffer[k, :4, :640])
            step_max = jnp.maximum(step_max, buffer[k, :, 640:])
        total = jnp.zeros((4, 640), F32)
        for k in range(count):
            total = total + buffer[k, 4:, :640] * jnp.exp2(
                (buffer[k, :4, :640] - largest) * scale2
            )
        return largest, total, step_max

    settle(stats)
    largest, total, step_max = merged(stat_plane, LANES)
    stat_ring[me_z, :, :640] = jnp.concatenate([largest, total], axis=0)
    stat_ring[me_z, :, 640:] = step_max
    stats = share(stat_ring, 1, me_z, ring_peer, NZ)
    hand_on(1, 1)
    hand_on(2, 1)
    for way in range(2):
        ring_arrived(way, 3, 1)
    plane_pack(1)
    plane_pack(7)
    plane_start(1)
    plane_start(7)
    hand_on(0, 2)

    settle(stats)
    row_max, row_total, step_max = merged(stat_ring, NZ)
    step_column = row_to_column(step_max[:1, :], STEP_ROWS)

    def decode_sum(c, carry):
        weighted, total = carry
        part = jnp.exp2((dl[c] - step_column) * scale2)
        for piece in range(8):
            total = total + part[:, piece * 128 : (piece + 1) * 128]
        chunk = values[pl.ds(c * 4, 4)].reshape(1024, 128)
        weighted = weighted + jnp.dot(part.astype(BF16), chunk, preferred_element_type=F32)
        return weighted, total

    nothing = jnp.zeros((STEP_ROWS, 128), F32)
    weighted, total = lax.fori_loop(0, 8, decode_sum, (nothing, nothing))
    sum_plane[me_lane, :STEP_ROWS, :] = weighted
    sum_plane[me_lane, STEP_ROWS:, :] = jnp.broadcast_to(
        column_to_row(jnp.sum(total, axis=1, keepdims=True)), (8, 128)
    )
    sums = share(sum_plane, 2, me_lane, plane_peer, LANES)
    hand_on(1, 2)
    for way in range(2):
        ring_arrived(way, 2, 2)
    plane_pack(2)
    plane_pack(6)
    plane_start(2)
    plane_start(6)
    hand_on(0, 3)

    settle(sums)
    total = sum_plane[0]
    for k in range(1, LANES):
        total = total + sum_plane[k]
    sum_ring[me_z] = total
    sums = share(sum_ring, 3, me_z, ring_peer, NZ)

    for g in range(4):
        factor = (
            jnp.exp2((chunk_max[g * 8 : g * 8 + 8, :] - row_max[g : g + 1]) * scale2)
            / row_total[g : g + 1]
        )
        high = factor.astype(BF16)
        low = (factor - high.astype(F32)).astype(BF16)
        rescale[g] = jnp.concatenate([high.astype(F32), low.astype(F32)], axis=0).astype(BF16)

    def importance(i, carry):
        g, c = i // 8, lax.rem(i, 8)
        found = contract_last(rescale[g], probs[i])
        wanted = lax.rem(lax.broadcasted_iota(I32, (16, 256), 0), 8) == c
        found = jnp.sum(jnp.where(wanted, found, 0.0), axis=0, keepdims=True)
        value = (LAMBDA * aux[16:17, :]) * found - (1.0 - LAMBDA) * redundancy[pl.ds(i, 1), :]
        redundancy[pl.ds(i, 1), :] = jnp.where(aux[pl.ds(c, 1), :] > 0.5, value, 0.0)
        return carry

    lax.fori_loop(0, 32, importance, 0)
    for g in range(4):
        for c in range(8):
            out_scores[g : g + 1, c * 256 : (c + 1) * 256] = redundancy[g * 8 + c : g * 8 + c + 1, :]

    for way in range(2):
        ring_arrived(way, 1, 3)
    plane_pack(3)
    plane_pack(5)
    plane_start(3)
    plane_start(5)

    settle(sums)
    total = sum_ring[0]
    for k in range(1, NZ):
        total = total + sum_ring[k]
    fresh = jnp.exp2((new_logits - step_column) * scale2)
    weighted = total[:STEP_ROWS] + jnp.dot(
        fresh.astype(BF16), new_values[...], preferred_element_type=F32
    )
    bottom = row_to_column(total[STEP_ROWS : STEP_ROWS + 1, :], STEP_ROWS)
    bottom = bottom + jnp.sum(fresh, axis=1, keepdims=True)
    out_decoded[...] = (weighted / bottom).astype(BF16)

    for way in range(2):
        ring_arrived(way, 0, 4)
    plane_pack(4)
    plane_start(4)

    for b in order:
        for i in range(1, LANES):
            plane_copies[b, i].wait_recv()

    def unpack(j, carry):
        at = picks[j]
        out_keys[j] = yr[at, 0]
        out_values[j] = yr[at, 1]
        return carry

    lax.fori_loop(0, out_keys.shape[0], unpack, 0)
    for b in order[-depth:]:
        for i in range(1, LANES):
            plane_copies[b, i].wait_send()
    for copy in ring_copies.values():
        copy.wait_send()


def build(slots, collective_id, scale2, keep):
    s1, s2, s3, s4 = slots
    slot = (2, 256, 128)

    def buffers(count):
        return pltpu.VMEM((count, *slot), BF16)

    vmem, smem = pl.BlockSpec(memory_space=pltpu.VMEM), pl.BlockSpec(memory_space=pltpu.SMEM)
    return pl.pallas_call(
        functools.partial(exchange, slots, scale2),
        out_shape=(
            jax.ShapeDtypeStruct((4, 2048), F32),
            jax.ShapeDtypeStruct((keep, 256, 128), BF16),
            jax.ShapeDtypeStruct((keep, 256, 128), BF16),
            jax.ShapeDtypeStruct((STEP_ROWS, 128), BF16),
        ),
        in_specs=[smem] * 4 + [vmem] * 10,
        out_specs=(vmem,) * 4,
        scratch_shapes=[
            buffers(s1),
            buffers(s1),
            buffers(s1),
            buffers(s2),
            buffers(s3),
            buffers(s1),
            buffers(s2),
            buffers(s3),
            buffers(2 * s4),
            pltpu.VMEM((4, LANES, *slot), BF16),
            buffers(NZ * LANES),
            pltpu.VMEM((8192, 128), F32),
            pltpu.VMEM((32, 256, 640), BF16),
            pltpu.VMEM((32, 640), F32),
            pltpu.VMEM((32, 640), F32),
            pltpu.VMEM((32, 256), F32),
            pltpu.VMEM((8, STEP_ROWS, 1024), F32),
            pltpu.VMEM((4, 16, 640), BF16),
            pltpu.VMEM((LANES, 8, 768), F32),
            pltpu.VMEM((NZ, 8, 768), F32),
            pltpu.VMEM((LANES, STEP_ROWS + 8, 128), F32),
            pltpu.VMEM((NZ, STEP_ROWS + 8, 128), F32),
            pltpu.SemaphoreType.DMA((2, 16)),
            pltpu.SemaphoreType.DMA((2, 16)),
            pltpu.SemaphoreType.DMA((NZ, LANES)),
            pltpu.SemaphoreType.DMA((NZ, LANES)),
            pltpu.SemaphoreType.DMA((4, 8)),
            pltpu.SemaphoreType.DMA((4, 8)),
        ],
        compiler_params=pltpu.CompilerParams(
            collective_id=collective_id,
            has_side_effects=True,
            vmem_limit_bytes=67_043_328,
        ),
        name="exchange_%d" % s1,
    )


def send_plan(keep_row, owner_row, me_z, me_lane):
    owners = jnp.arange(NZ * LANES, dtype=I32)
    match = owner_row[None, :] == owners[:, None]
    has = jnp.any(match, axis=1).astype(I32).reshape(NZ, LANES)
    block = jnp.sum(jnp.where(match, keep_row[None, :], 0), axis=1).reshape(NZ, LANES)
    turn = (lax.broadcasted_iota(I32, (NZ, NZ), 0) + me_z) % NZ == lax.broadcasted_iota(
        I32, (NZ, NZ), 1
    )
    has = jnp.sum(jnp.where(turn[:, :, None], has[None], 0), axis=1)
    block = jnp.sum(jnp.where(turn[:, :, None], block[None], 0), axis=1)
    lower = (
        lax.broadcasted_iota(I32, (LANES, LANES), 0) < lax.broadcasted_iota(I32, (LANES, LANES), 1)
    )
    rank = jnp.sum(jnp.where(lower[None], has[:, :, None], 0), axis=1)
    count = jnp.sum(has, axis=1)
    n4 = count[HALF]
    ahead = count[1] + count[2] + count[3]
    behind = count[7] + count[6] + count[5]
    first = jnp.clip((n4 + behind - ahead + 1) // 2, jnp.maximum(n4 - 4, 0), jnp.minimum(n4, 4))
    tails_p = [first]
    tails_m = [n4 - first]
    for k in (3, 2, 1):
        tails_p.append(tails_p[-1] + count[k])
        tails_m.append(tails_m[-1] + count[NZ - k])
    tails = jnp.maximum(jnp.stack(tails_p[::-1]), jnp.stack(tails_m[::-1]))
    start = jnp.stack(
        [
            jnp.zeros((), I32),
            tails_p[2],
            tails_p[1],
            tails_p[0],
            jnp.zeros((), I32),
            tails_m[0],
            tails_m[1],
            tails_m[2],
        ]
    )
    position = start[:, None] + rank
    far = lax.broadcasted_iota(I32, (NZ, LANES), 0) == HALF
    k_of = lax.broadcasted_iota(I32, (NZ, LANES), 0)
    over = far & (rank >= first)
    position = jnp.where(over, rank - first, position)
    way = (k_of > HALF) | over
    used = (has > 0) & (k_of > 0)
    return has, block, position, way, used, tails


def shards(
    stored_keys,
    stored_values,
    observed_queries,
    decoded_queries,
    step_keys,
    decoded_values,
    keep_lists,
    owner_ids,
    cache_length,
):
    tokens, head_count, width = stored_keys.shape
    window = observed_queries.shape[0]
    group = observed_queries.shape[1] // head_count
    step_count = decoded_queries.shape[0]
    keep = keep_lists.shape[1]
    scale2 = math.log2(math.e) / math.sqrt(width)
    me_z = lax.axis_index("ctx_0")
    me_lane = lax.axis_index("ctx_1") * 2 + lax.axis_index("ctx_2")
    rank = me_z * LANES + me_lane
    keep_row, owner_row = keep_lists[0], owner_ids[0]

    has, block, position, way, used, tails = send_plan(keep_row, owner_row, me_z, me_lane)
    slot_numbers = jnp.arange(FITS_ALL[0], dtype=I32)
    lists = jnp.stack(
        [
            jnp.sum(
                jnp.where(
                    (used & (way == bool(w)))[None] & (position[None] == slot_numbers[:, None, None]),
                    block[None],
                    0,
                ),
                axis=(1, 2),
            )
            for w in range(2)
        ]
    )
    coded = jnp.where(has > 0, position + 1 + jnp.where((way & (position >= 0)), 32, 0), 0)
    back = (lax.broadcasted_iota(I32, (NZ, NZ), 0) + (NZ - me_z)) % NZ == lax.broadcasted_iota(
        I32, (NZ, NZ), 1
    )
    coded = jnp.sum(jnp.where(back[:, :, None], coded[None], 0), axis=1)
    row = jnp.concatenate([coded, jnp.broadcast_to(tails[None], (NZ, 4))], axis=1)
    row = jnp.broadcast_to(row[None, :, None, :], (2, NZ, LANES, 12)).reshape(2 * NZ * LANES, 12)
    got = lax.all_to_all(row, BATCH_CTX, 0, 0, tiled=True)
    most = jnp.max(got[:, LANES:], axis=0)
    mine = lax.dynamic_slice(got, (lax.axis_index("batch") * (NZ * LANES), 0), (NZ * LANES, LANES))
    valid = lax.dynamic_slice(mine, (0, me_lane), (NZ * LANES, 1))[:, 0] > 0
    before = jnp.arange(NZ * LANES)[:, None] < jnp.arange(NZ * LANES)[None, :]
    order = jnp.sum((before & valid[:, None]).astype(I32), axis=0)
    chosen = valid[None, :] & (order[None, :] == jnp.arange(keep, dtype=I32)[:, None])
    picks = jnp.sum(jnp.where(chosen, jnp.arange(NZ * LANES, dtype=I32)[None, :], 0), axis=1)
    my_ring = lax.dynamic_slice(
        mine.reshape(NZ, LANES, LANES), (0, me_lane, 0), (NZ, 1, LANES)
    )[:, 0]
    steps_back = (me_z + NZ - lax.broadcasted_iota(I32, (NZ, NZ), 0)) % NZ == lax.broadcasted_iota(
        I32, (NZ, NZ), 1
    )
    ring_rows = jnp.sum(jnp.where(steps_back[:, :, None], my_ring[None], 0), axis=1)

    seq = cache_length[0]
    base = rank * tokens
    local_live = (seq - base).reshape(1)
    at = base + jnp.arange(tokens, dtype=I32)
    live = (at < seq).astype(F32).reshape(8, 256)
    in_block = jnp.clip(seq - at // BLOCK * BLOCK, 0, BLOCK).astype(F32).reshape(8, 256)
    factor = jnp.broadcast_to(
        (seq.astype(F32) / (window * group)).reshape(1, 1), (8, 256)
    )
    aux = jnp.concatenate([live, jnp.maximum(in_block - 1.0, 1.0), factor], axis=0)
    blocks = tokens // BLOCK
    wide = jnp.arange(tokens * head_count, dtype=I32)
    kept = jnp.any(keep_row[None, :] == (wide // (BLOCK * head_count))[:, None], axis=1)
    kept_bias = jnp.where(kept & (base + wide // head_count < seq), 0.0, FAR).reshape(8, 1024)
    row_of = jnp.arange(STEP_ROWS, dtype=I32)[:, None]
    lane_of = jnp.arange(128, dtype=I32)[None, :]
    row_head, row_step = row_of // (step_count * group), row_of % (step_count * group) // group
    same_head = lane_of % head_count == row_head
    head_bias = jnp.where(same_head, 0.0, FAR).astype(F32)
    new_bias = jnp.where(
        same_head & (lane_of // head_count <= row_step) & (lane_of < step_count * head_count),
        0.0,
        FAR,
    ).astype(F32)

    def by_head(q):
        n = q.shape[0]
        q = q.reshape(n, head_count, group, width).transpose(1, 0, 2, 3)
        return q.reshape(head_count, n * group, width)

    queries = by_head(observed_queries)
    step_queries = by_head(decoded_queries).reshape(STEP_ROWS, width)

    def padded(rows):
        flat = rows.reshape(step_count * head_count, width)
        return jnp.pad(flat, ((0, 128 - step_count * head_count), (0, 0)))

    new_keys, new_values = padded(step_keys), padded(decoded_values)
    key_blocks = stored_keys.reshape(blocks, BLOCK * head_count, width)
    value_blocks = stored_values.reshape(blocks, BLOCK * head_count, width)

    def run(slots, collective_id):
        def call():
            second = ring_rows > 32
            place = jnp.where(second, ring_rows - 33, jnp.maximum(ring_rows - 1, 0))
            is_far = lax.broadcasted_iota(I32, (NZ, LANES), 0) == HALF
            place = place + jnp.where(second & is_far, slots[3], 0)
            is_own = lax.broadcasted_iota(I32, (NZ, LANES), 0) == 0
            own = lax.broadcast_in_dim(block[0], (NZ, LANES), (1,))
            table = jnp.where(is_own, own, place)
            return build(slots, collective_id, scale2, keep)(
                table,
                lists,
                picks,
                local_live,
                key_blocks,
                value_blocks,
                queries,
                step_queries,
                new_keys,
                new_values,
                kept_bias,
                head_bias,
                new_bias,
                aux,
            )

        return call

    fits = jnp.all(most <= jnp.array(FITS_MOST, I32))
    scores, kept_keys, kept_values, decoded = lax.cond(
        fits, run(FITS_MOST, 0), run(FITS_ALL, 1)
    )
    decoded = (
        decoded.reshape(head_count, step_count, group, width)
        .transpose(1, 0, 2, 3)
        .reshape(step_count, head_count * group, width)
    )
    shape = (keep * BLOCK, head_count, width)
    return scores, kept_keys.reshape(shape), kept_values.reshape(shape), decoded


def solution(mesh):
    split = Mesh(
        mesh.devices.reshape(mesh.shape["batch"], 8, 4, 2, mesh.shape["head"]),
        ("batch", "ctx_0", "ctx_1", "ctx_2", "head"),
    )
    return jax.shard_map(
        shards,
        mesh=split,
        in_specs=(
            P(BATCH_CTX, "head", None),
            P(BATCH_CTX, "head", None),
            P("batch", "head", None),
            P("batch", "head", None),
            P("batch", "head", None),
            P("batch", "head", None),
            P(BATCH_CTX, None),
            P(BATCH_CTX, None),
            P("batch"),
        ),
        out_specs=(
            P(("batch", "head"), CTX),
            P(BATCH_CTX, "head", None),
            P(BATCH_CTX, "head", None),
            P("batch", "head", None),
        ),
        check_vma=False,
    )
```

time: 414 us -> 230 us (0.56); the launches traced: 406 us -> 230 us
  blocking collectives: 186 us -> 0 us
  Pallas kernels: 0 us -> 166 us
  waiting for transfers between devices: 61.2 us -> 8.38 us
  local copies, waits for them, and re-layouts: 51.5 us -> 15.5 us
  matrix products: 30.9 us -> 0 us
  starting transfers between devices: 43.7 us -> 14.9 us
  other arithmetic: 30.1 us -> 11.6 us
  between operations: 2.34 us -> 12.2 us
    pallas_call x0 -> x1, Pallas kernels: none -> 166 us  [call(): build(slots, collective_id, scale2, keep)]
    all_to_all x1 -> x0, blocking collectives: 105 us -> none  [shards(): lax.all_to_all(send_keys.reshape(ctx_count, capacity, BLOCK_TOKENS, head_...]
    all_gather x3 -> x0, blocking collectives: 81.5 us -> none  [gathered_once(): both, at, found = (lax.all_gather(jnp.concatenate(lines), axis), 0, {})]
    all_to_all x5 -> x1, waiting for transfers between devices: 61.2 us -> 8.38 us  [shards(): got = lax.all_to_all(row, BATCH_CTX, 0, 0, tiled=True)]
    dot_general x10 -> x0, matrix products: 30.9 us -> none  [the longest x4 16.1 us: shards(): jnp.einsum('wrd,td->wrt', grouped[:, head_index], stored_keys[:, head_ind...]
    gather x9 -> x0, local copies, waits for them, and re-layouts: 30.6 us -> none  [the longest x1 7.88 us: shards(): blocked_keys[slot_block]]
    all_to_all x5 -> x1, starting transfers between devices: 43.7 us -> 14.9 us  [shards(): got = lax.all_to_all(row, BATCH_CTX, 0, 0, tiled=True)]
    reduce_sum x9 -> x8, other arithmetic: 17.9 us -> 2.14 us  [the longest x1 0.76 us: send_plan(): jnp.sum(jnp.where(match, keep_row[None, :], 0), axis=1).reshape(NZ, LANES)]
  transfers between devices with their start and end apart: 5 -> 1, of which waited for: 3 -> 1; matrix products, arithmetic and copies ran while one was open for 24% -> 1% of each run, Pallas kernels for 0% -> 0%
where the time goes in v2:
time: 230 us
  Pallas kernels  166 us (72%)
  local copies, waits for them, and re-layouts  15.5 us (7%)
  starting transfers between devices  14.9 us (6%)
  between operations  12.2 us (5%)
  other arithmetic  11.6 us (5%)
  waiting for transfers between devices  8.38 us (4%)
    pallas_call x1, Pallas kernels, call(): build(slots, collective_id, scale2, keep)  166 us
    all_to_all x1, starting transfers between devices, shards(): got = lax.all_to_all(row, BATCH_CTX, 0, 0, tiled=True)  14.9 us
    all_to_all x1, waiting for transfers between devices, shards(): got = lax.all_to_all(row, BATCH_CTX, 0, 0, tiled=True)  8.38 us
    unnamed x5, local copies, waits for them, and re-layouts  5.35 us
  transfers between devices with their start and end apart: 1, of which 1 were waited for; matrix products, arithmetic and copies ran while one was open for 1% of the time, Pallas kernels for 0%

profile of v2, /device:TPU:1, one launch (start us, length us, event | category | flops | bytes accessed | tf_op | source)
XLA Modules:
  0.0 229.5 jit_solution(12763874040918020741)
XLA Ops:
  0.7 0.7 fusion.27
  1.5 0.8 select_reduce_fusion.11
  2.8 0.6 fusion.45
  14.8 14.9 %all-to-all-start = ((s32[128,1,12]{2,1,0:T(1,128)}), s32[128,1,12]{2,1,0:T(1,128)S(1)}, u32[]{:S(2)}, u32[]{:S(2)}) async-start(s32[128,1,12]{2,1,0:T(1,128)} %bitcast.16), calls=%async_computation | async-start | bytes 131072 | tf_op jit(solution)/shard_map/all_to_all | solution.py:567
  31.3 0.7 maximum_maximum_fusion
  32.0 8.4 %all-to-all-done = s32[128,1,12]{2,1,0:T(1,128)S(1)} async-done(((s32[128,1,12]{2,1,0:T(1,128)}), s32[128,1,12]{2,1,0:T(1,128)S(1)}, u32[]{:S(2)}, u32[]{:S(2)}) %all-to-all-start) | async-done | bytes 6176 | tf_op jit(solution)/shard_map/all_to_all | solution.py:567
  40.5 1.3 compare_reduce_fusion.3
  42.5 1.3 compare_reduce_fusion.2
  44.0 178.8 %conditional.1 = ((f32[4,2048]{1,0:T(4,128)}, bf16[26,256,128]{2,1,0:T(8,128)(2,1)}, bf16[26,256,128]{2,1,0:T(8,128)(2,1)}, bf16[80,128]{1,0:T(8,128)(2,1)})) conditional(s32[]{:T(128)} %convert_element_type.32, (s32[8,8]{1,0:T(8,128)S(1)}, pred[8]{0:T(512)(128)(4,1)S(1)}, s32[8]{0:T(128)S(1)}, s32[8]{0:T(128)S(1)}, ...), branch_computations={%region_11.16_spmd.clone, %region_16.21_spmd.clone} | conditional | flops 683095 | bytes 3303196 | solution.py:653
  45.3 0.6 select_reduce_fusion.3.picks
  46.6 0.7 add_select_fusion.3.table
  47.4 0.9 compare_reduce_fusion.1
  48.2 1.3 and_select_fusion.5.kept_bias
  49.5 1.3 pad.22.new_values
  50.8 1.3 pad.21.new_keys
  52.1 0.7 copy.92
  53.5 0.7 fusion.12
  54.2 1.6 copy.91
  55.8 0.9 copy.82.queries
  56.7 166.1 %exchange_17.2 = (f32[4,2048]{1,0:T(4,128)}, bf16[26,256,128]{2,1,0:T(8,128)(2,1)}, bf16[26,256,128]{2,1,0:T(8,128)(2,1)}, bf16[80,128]{1,0:T(8,128)(2,1)}) custom-call(s32[8,8]{1,0:T(8,128)} %add_select_fusion.3.table, s32[2,26]{1,0:T(2,128)} %get-tuple-element.1167.lists, s32[26]{0:T(128)} %select_reduce_fusion.3.picks, s32[1]{0:T(128)} %bitcast.50.local_live, ...), custom_call_target="tpu_custom_call" | custom-call | tf_op jit(solution)/shard_map/cond/branch_1_fun/exchange_17/pallas_call | solution.py:633
  222.8 0.7 reshape.686
  224.2 1.4 copy.108
  225.5 2.8 %copy.109 = bf16[1664,4,128]{2,1,0:T(4,128)(2,1)} copy(bf16[1664,4,128]{2,1,0:T(4,128)(2,1)} %bitcast.87) | data formatting | bytes 3407872
  228.3 1.2 copy.110
  (78 shorter events, 5.5 us)
Async XLA Ops:
  14.8 25.6 %all-to-all-start = ((s32[128,1,12]{2,1,0:T(1,128)}), s32[128,1,12]{2,1,0:T(1,128)S(1)}, u32[]{:S(2)}, u32[]{:S(2)}) async-start(s32[128,1,12]{2,1,0:T(1,128)} %bitcast.16), calls=%async_computation | async-start | bytes 131072 | tf_op jit(solution)/shard_map/all_to_all | solution.py:567
  225.5 2.8 %copy-start = (bf16[26,256,128]{2,1,0:T(8,128)(2,1)S(1)}, bf16[26,256,128]{2,1,0:T(8,128)(2,1)}, u32[]{:S(2)}) copy-start(bf16[26,256,128]{2,1,0:T(8,128)(2,1)} %get-tuple-element.1898) | copy-start | bytes 5111812

commit v3 on v2

v3 whole, which is shorter than its diff:
```python
import functools
import math

import jax
import jax.numpy as jnp
from jax import lax
from jax.experimental import pallas as pl
from jax.experimental.pallas import tpu as pltpu
from jax.sharding import Mesh
from jax.sharding import PartitionSpec as P

BLOCK = 64
CTX = ("ctx_0", "ctx_1", "ctx_2")
BATCH_CTX = ("batch", "ctx_0", "ctx_1", "ctx_2")
MESH = pl.DeviceIdType.MESH
FAR = -1e30
LAMBDA = 0.1
NORM_EPS = 1e-06
NZ = 8
LANES = 8
HALF = NZ // 2
HEADS = 4
GROUP = 5
STEPS = 4
HEAD_ROWS = HEADS * GROUP
STEP_ROWS = STEPS * HEAD_ROWS
WINDOW = 128
KEEP = 26
BLOCKS = 32
SECOND = 32
FITS_ALL = (26, 20, 12, 4)
FITS_MOST = (17, 13, 10, 4)
F32, BF16, I32 = jnp.float32, jnp.bfloat16, jnp.int32


def contract_last(a, b):
    return lax.dot_general(a, b, (((1,), (1,)), ((), ())), preferred_element_type=F32)


def row_to_column(row, rows):
    return jnp.transpose(jnp.broadcast_to(row, (128, 128)))[:rows, :1]


def column_to_row(column):
    rows = column.shape[0]
    wide = jnp.concatenate(
        [jnp.broadcast_to(column, (rows, 128)), jnp.zeros((128 - rows, 128), F32)], axis=0
    )
    return jnp.transpose(wide)[:1, :]


def plan(keep, owner, lists, own, kept, meta, block_of):
    me_z = lax.axis_index("ctx_0")
    for o in range(NZ * LANES):
        block_of[o] = -1
    for b in range(BLOCKS):
        kept[b] = 0
    for slot in range(SECOND):
        lists[0, slot] = 0
        lists[1, slot] = 0

    def place(j, carry):
        block_of[owner[0, j]] = keep[0, j]
        kept[keep[0, j]] = 1
        return carry

    lax.fori_loop(0, KEEP, place, 0)
    planes = [lax.rem(me_z + k, NZ) for k in range(NZ)]
    blocks = [[block_of[planes[k] * LANES + i] for i in range(LANES)] for k in range(NZ)]
    has = [[(b >= 0).astype(I32) for b in row] for row in blocks]
    count = [sum(row[1:], row[0]) for row in has]
    n4 = count[HALF]
    ahead, behind = count[1] + count[2] + count[3], count[7] + count[6] + count[5]
    first = lax.max(n4 - 4, lax.min(lax.min(n4, 4), lax.max(0, (n4 + behind - ahead + 1) >> 1)))
    first = lax.max(first, 0)
    second = n4 - first
    tails_p = [first, first + count[3], first + count[3] + count[2], first + ahead]
    tails_m = [second, second + count[5], second + count[5] + count[6], second + behind]
    start = [0, tails_p[2], tails_p[1], tails_p[0], 0, tails_m[0], tails_m[1], tails_m[2]]
    needs = [lax.max(p, m) for p, m in zip(tails_p[::-1], tails_m[::-1])]
    for k in range(NZ):
        rank = start[k] + jnp.zeros((), I32)
        for i in range(LANES):
            if k == HALF:
                way = (rank >= first).astype(I32)
                slot = rank - way * first
            else:
                way = jnp.full((), int(k > HALF), I32)
                slot = rank
            there = has[k][i]
            meta[planes[k], i] = there * (slot + 1 + way * SECOND)
            if k == 0:
                own[i] = lax.max(blocks[k][i], 0)
            else:

                @pl.when(there > 0)
                def _(way=way, slot=slot, block=blocks[k][i]):
                    lists[way, slot] = block

            rank = rank + there
        for n in range(4):
            meta[k, LANES + n] = needs[n]


def exchange(
    slots,
    scale2,
    lists,
    own,
    kept,
    length,
    meta,
    keys,
    values,
    queries,
    step_queries,
    new_keys,
    new_values,
    out_scores,
    out_decoded,
    out_meta,
    out_needs,
    yr_k,
    yr_v,
    zs_p,
    zs_m,
    zr_p1,
    zr_p2,
    zr_p3,
    zr_m1,
    zr_m2,
    zr_m3,
    zr_4,
    yb,
    kf,
    probs,
    chunk_max,
    chunk_sum,
    redundancy,
    dl,
    rescale,
    meta_ring,
    needs_pair,
    table,
    stat_plane,
    stat_ring,
    sum_plane,
    sum_ring,
    z_send,
    z_recv,
    y_send,
    y_recv,
    s_send,
    s_recv,
    t_sem,
):
    me_b = lax.axis_index("batch")
    me_z = lax.axis_index("ctx_0")
    me_lane = lax.axis_index("ctx_1") * 2 + lax.axis_index("ctx_2")
    s1, s2, s3, s4 = slots
    stores = (keys, values)
    results = (yr_k, yr_v)

    def ring_peer(k):
        return {"ctx_0": lax.rem(me_z + (k + NZ), NZ)}

    def plane_peer(i):
        lane = lax.rem(me_lane + i, LANES)
        return {"ctx_1": lane // 2, "ctx_2": lax.rem(lane, 2)}

    def pair_peer(i):
        return {"batch": 1 - me_b}

    barrier = pltpu.get_barrier_semaphore()
    for i in range(1, LANES):
        pl.semaphore_signal(barrier, inc=1, device_id=plane_peer(i), device_id_type=MESH)
    for k in range(1, NZ):
        pl.semaphore_signal(barrier, inc=1, device_id=ring_peer(k), device_id_type=MESH)
    pl.semaphore_signal(barrier, inc=1, device_id=pair_peer(0), device_id_type=MESH)

    def pack_lists(slot, carry):
        for way, dst in ((0, zs_p), (1, zs_m)):
            at = lists[way, slot]
            for kind in range(2):
                dst[kind][slot] = stores[kind][at]
        return carry

    lax.fori_loop(0, s1, pack_lists, 0)
    for i in range(LANES):
        at = own[lax.rem(me_lane + i, LANES)]
        for kind in range(2):
            yb[kind, 0, i] = stores[kind][at]
    meta_ring[me_z] = meta[me_z]

    pl.semaphore_wait(barrier, LANES - 1 + NZ - 1 + 1)

    def share(source, buffer, number, at, peer, count):
        copies = []
        for i in range(1, count):
            copy = pltpu.make_async_remote_copy(
                src_ref=source(i),
                dst_ref=buffer.at[at],
                send_sem=s_send.at[number, i],
                recv_sem=s_recv.at[number, i],
                device_id=peer(i),
                device_id_type=MESH,
            )
            copy.start()
            copies.append(copy)
        return copies

    def settle(copies):
        for copy in copies:
            copy.wait()

    metas = share(
        lambda k: meta.at[lax.rem(me_z + k, NZ)], meta_ring, 4, me_z, ring_peer, NZ
    )

    segments = ((0, s4), (s4, s3), (s3, s2), (s2, s1))
    ring = ((zs_p, zr_p1, zr_p2, zr_p3), (zs_m, zr_m1, zr_m2, zr_m3))
    ring_copies = {}

    def ring_start(kind, way, q, hop):
        a, b = segments[q]
        if a == b:
            return
        src = ring[way][hop - 1][kind].at[pl.ds(a, b - a)]
        if hop < HALF:
            dst = ring[way][hop][kind].at[pl.ds(a, b - a)]
        else:
            dst = zr_4[kind].at[pl.ds(way * s4 + a, b - a)]
        number = q * HALF + hop - 1
        copy = pltpu.make_async_remote_copy(
            src_ref=src,
            dst_ref=dst,
            send_sem=z_send.at[kind, way, number],
            recv_sem=z_recv.at[kind, way, number],
            device_id=ring_peer(1 if way == 0 else -1),
            device_id_type=MESH,
        )
        copy.start()
        ring_copies[kind, way, q, hop] = copy

    def arrived(kind, q, hop):
        for way in range(2):
            if (kind, way, q, hop) in ring_copies:
                ring_copies[kind, way, q, hop].wait_recv()

    def hand_on(kind, hop):
        for q in range(HALF - hop):
            for way in range(2):
                if (kind, way, q, hop) in ring_copies:
                    ring_copies[kind, way, q, hop].wait_recv()
                ring_start(kind, way, q, hop + 1)
        arrived(kind, HALF - hop, hop)

    arrivals = {1: zr_p1, 2: zr_p2, 3: zr_p3, 4: zr_4, 5: zr_m3, 6: zr_m2, 7: zr_m1}
    plane_copies = {}

    def plane_pack(kind, b):
        source = lax.rem(me_z + (NZ - b), NZ)
        got = arrivals[b][kind]
        for i in range(LANES):
            code = table[source, 0, lax.rem(me_lane + i, LANES)]
            is_second = (code > SECOND).astype(I32)
            slot = lax.max(code - 1 - is_second * SECOND, 0)
            if b == HALF:
                slot = lax.min(slot, s4 - 1) + is_second * s4
            else:
                slot = lax.min(slot, got.shape[0] - 1)
            yb[kind, b, i] = got[slot]

    def plane_start(kind, b):
        source = lax.rem(me_z + (NZ - b), NZ) * LANES + me_lane
        for i in range(1, LANES):
            copy = pltpu.make_async_remote_copy(
                src_ref=yb.at[kind, b, i],
                dst_ref=results[kind].at[source],
                send_sem=y_send.at[kind, b, i],
                recv_sem=y_recv.at[kind, b, i],
                device_id=plane_peer(i),
                device_id_type=MESH,
            )
            copy.start()
            plane_copies[kind, b, i] = copy
        copy = pltpu.make_async_copy(
            yb.at[kind, b, 0], results[kind].at[source], y_send.at[kind, b, 0]
        )
        copy.start()
        plane_copies[kind, b, 0] = copy

    def across(kind, *batches):
        for b in batches:
            plane_pack(kind, b)
        for b in batches:
            plane_start(kind, b)

    for kind in range(2):
        for q in range(HALF):
            for way in range(2):
                ring_start(kind, way, q, 1)
    plane_start(0, 0)
    plane_start(1, 0)

    def widen(c, carry):
        kf[pl.ds(pl.multiple_of(c * 256, 256), 256), :] = keys[c].astype(F32)
        return carry

    lax.fori_loop(0, BLOCKS, widen, 0)
    live_here = length[0] - (me_z * LANES + me_lane) * (BLOCKS * BLOCK)
    rows = lax.broadcasted_iota(I32, (256, 256), 0)
    columns = lax.broadcasted_iota(I32, (256, 256), 1)
    lane_256 = lax.broadcasted_iota(I32, (1, 256), 1)

    def score(i, carry):
        g, c = i // 8, lax.rem(i, 8)
        chunk = kf[pl.ds(c * 1024 + g, 256, stride=4), :].astype(BF16)
        live = lax.broadcasted_iota(I32, (256, 128), 0) + c * 256 < live_here
        bias = jnp.where(live, 0.0, FAR)
        logits = contract_last(chunk, queries[g]) + jnp.concatenate([bias] * 5, axis=1)
        largest = jnp.max(logits, axis=0, keepdims=True)
        weights = jnp.exp2((logits - largest) * scale2)
        chunk_max[pl.ds(i, 1), :] = largest
        chunk_sum[pl.ds(i, 1), :] = jnp.sum(weights, axis=0, keepdims=True)
        probs[i] = weights.astype(BF16)
        gram = contract_last(chunk, chunk)
        on_diagonal = jnp.where(rows == columns, gram, 0.0)
        squares = jnp.sum(on_diagonal, axis=0, keepdims=True)
        down = jnp.sum(on_diagonal, axis=1, keepdims=True)
        spread = jnp.where(live[:, :1], 1.0, 0.0) / jnp.sqrt(down + NORM_EPS)
        norm = jnp.sqrt(squares + NORM_EPS)
        together = jnp.where(rows // BLOCK == columns // BLOCK, gram, 0.0)
        row_sum = jnp.sum(together * spread, axis=0, keepdims=True) / norm
        live_lanes = jnp.where(lane_256 + c * 256 < live_here, 1.0, 0.0)
        own_term = live_lanes * squares / (norm * norm)
        in_block = jnp.clip(live_here - c * 256 - lane_256 // BLOCK * BLOCK, 0, BLOCK).astype(F32)
        redundancy[pl.ds(i, 1), :] = (row_sum - own_term) / jnp.maximum(in_block - 1.0, 1.0)
        return carry

    lax.fori_loop(0, HEADS * 8, score, 0)

    row_of = lax.broadcasted_iota(I32, (STEP_ROWS, 128), 0)
    lane_of = lax.broadcasted_iota(I32, (STEP_ROWS, 128), 1)
    row_step = row_of % STEPS
    row_head = jnp.zeros((STEP_ROWS, 128), I32)
    for g in range(1, HEADS):
        row_head = row_head + (row_of >= g * GROUP * STEPS).astype(I32)
    same_head = lane_of % HEADS == row_head
    head_bias = jnp.concatenate([jnp.where(same_head, 0.0, FAR)] * 8, axis=1)
    may_see = same_head & (lane_of // HEADS <= row_step) & (lane_of < STEPS * HEADS)
    new_bias = jnp.where(may_see, 0.0, FAR)

    def padded(ref):
        return jnp.concatenate([ref[...], jnp.zeros((128 - STEPS * HEADS, 128), BF16)], axis=0)

    def decode_logits(c, top):
        chunk = keys[pl.ds(c * 4, 4)].reshape(1024, 128)
        kept_part = jnp.concatenate(
            [
                jnp.where(jnp.full((1, 256), kept[c * 4 + part], I32) > 0, 0.0, FAR)
                for part in range(4)
            ],
            axis=1,
        )
        token = lax.broadcasted_iota(I32, (1, 1024), 1) // HEADS + c * 256
        bias = kept_part + jnp.where(token < live_here, 0.0, FAR)
        found = contract_last(step_queries[...], chunk) + head_bias + bias
        dl[c] = found
        for part in range(8):
            top = jnp.maximum(top, found[:, part * 128 : (part + 1) * 128])
        return top

    new_logits = contract_last(step_queries[...], padded(new_keys)) + new_bias
    top = lax.fori_loop(0, 8, decode_logits, new_logits)
    step_top = column_to_row(jnp.max(top, axis=1, keepdims=True))

    maxima, sums = [], []
    for g in range(HEADS):
        part_max = chunk_max[g * 8 : g * 8 + 8, :]
        largest = jnp.max(part_max, axis=0, keepdims=True)
        maxima.append(largest)
        sums.append(
            jnp.sum(
                chunk_sum[g * 8 : g * 8 + 8, :] * jnp.exp2((part_max - largest) * scale2),
                axis=0,
                keepdims=True,
            )
        )
    stat_plane[me_lane, :, :640] = jnp.concatenate(maxima + sums, axis=0)
    stat_plane[me_lane, :, 640:] = jnp.broadcast_to(step_top, (8, 128))

    settle(metas)
    to_scalars = pltpu.make_async_copy(meta_ring, table, t_sem)
    to_scalars.start()
    to_scalars.wait()
    out_meta[me_lane] = meta_ring[...]
    stats = share(lambda i: stat_plane.at[me_lane], stat_plane, 0, me_lane, plane_peer, LANES)
    metas = share(lambda i: meta_ring, out_meta, 5, me_lane, plane_peer, LANES)

    def merged(buffer, count):
        largest = buffer[0, :4, :640]
        step_max = buffer[0, :, 640:]
        for k in range(1, count):
            largest = jnp.maximum(largest, buffer[k, :4, :640])
            step_max = jnp.maximum(step_max, buffer[k, :, 640:])
        total = jnp.zeros((4, 640), F32)
        for k in range(count):
            total = total + buffer[k, 4:, :640] * jnp.exp2(
                (buffer[k, :4, :640] - largest) * scale2
            )
        return largest, total, step_max

    settle(stats)
    largest, total, step_max = merged(stat_plane, LANES)
    stat_ring[me_z, :, :640] = jnp.concatenate([largest, total], axis=0)
    stat_ring[me_z, :, 640:] = step_max
    stats = share(lambda k: stat_ring.at[me_z], stat_ring, 1, me_z, ring_peer, NZ)
    hand_on(0, 1)
    across(0, 1, 7)
    settle(metas)
    most = out_meta[0, 0]
    for lane in range(LANES):
        for z in range(NZ):
            most = jnp.maximum(most, out_meta[lane, z])
    needs_pair[me_b] = most
    pair = share(lambda i: needs_pair.at[me_b], needs_pair, 6, me_b, pair_peer, 2)
    hand_on(1, 1)
    across(1, 1, 7)

    settle(stats)
    row_max, row_total, step_max = merged(stat_ring, NZ)
    step_column = row_to_column(step_max[:1, :], STEP_ROWS)

    def decode_sum(c, carry):
        weighted, total = carry
        part = jnp.exp2((dl[c] - step_column) * scale2)
        for piece in range(8):
            total = total + part[:, piece * 128 : (piece + 1) * 128]
        chunk = values[pl.ds(c * 4, 4)].reshape(1024, 128)
        weighted = weighted + jnp.dot(part.astype(BF16), chunk, preferred_element_type=F32)
        return weighted, total

    nothing = jnp.zeros((STEP_ROWS, 128), F32)
    weighted, total = lax.fori_loop(0, 8, decode_sum, (nothing, nothing))
    sum_plane[me_lane, :STEP_ROWS, :] = weighted
    sum_plane[me_lane, STEP_ROWS:, :] = jnp.broadcast_to(
        column_to_row(jnp.sum(total, axis=1, keepdims=True)), (8, 128)
    )
    sums = share(lambda i: sum_plane.at[me_lane], sum_plane, 2, me_lane, plane_peer, LANES)
    hand_on(0, 2)
    across(0, 2, 6)
    settle(sums)
    total = sum_plane[0]
    for k in range(1, LANES):
        total = total + sum_plane[k]
    sum_ring[me_z] = total
    sums = share(lambda k: sum_ring.at[me_z], sum_ring, 3, me_z, ring_peer, NZ)
    hand_on(1, 2)
    across(1, 2, 6)

    for g in range(HEADS):
        factor = (
            jnp.exp2((chunk_max[g * 8 : g * 8 + 8, :] - row_max[g : g + 1]) * scale2)
            / row_total[g : g + 1]
        )
        high = factor.astype(BF16)
        low = (factor - high.astype(F32)).astype(BF16)
        rescale[g] = jnp.concatenate([high.astype(F32), low.astype(F32)], axis=0).astype(BF16)
    share_of_row = jnp.full((1, 256), length[0], I32).astype(F32) / (WINDOW * GROUP)

    def importance(i, carry):
        g, c = i // 8, lax.rem(i, 8)
        found = contract_last(rescale[g], probs[i])
        wanted = lax.rem(lax.broadcasted_iota(I32, (16, 256), 0), 8) == c
        found = jnp.sum(jnp.where(wanted, found, 0.0), axis=0, keepdims=True)
        value = (LAMBDA * share_of_row) * found - (1.0 - LAMBDA) * redundancy[pl.ds(i, 1), :]
        live = lane_256 + c * 256 < live_here
        redundancy[pl.ds(i, 1), :] = jnp.where(live, value, 0.0)
        return carry

    lax.fori_loop(0, HEADS * 8, importance, 0)
    for g in range(HEADS):
        for c in range(8):
            out_scores[g : g + 1, c * 256 : (c + 1) * 256] = redundancy[g * 8 + c : g * 8 + c + 1, :]
    settle(pair)
    out_needs[...] = jnp.maximum(needs_pair[0], needs_pair[1])

    hand_on(0, 3)
    across(0, 3, 5)
    hand_on(1, 3)
    across(1, 3, 5)

    settle(sums)
    total = sum_ring[0]
    for k in range(1, NZ):
        total = total + sum_ring[k]
    fresh = jnp.exp2((new_logits - step_column) * scale2)
    weighted = total[:STEP_ROWS] + jnp.dot(
        fresh.astype(BF16), padded(new_values), preferred_element_type=F32
    )
    bottom = row_to_column(total[STEP_ROWS : STEP_ROWS + 1, :], STEP_ROWS)
    bottom = bottom + jnp.sum(fresh, axis=1, keepdims=True)
    out_decoded[...] = (weighted / bottom).astype(BF16)

    for kind in range(2):
        arrived(kind, 0, HALF)
        across(kind, HALF)

    for (kind, b, i), copy in plane_copies.items():
        copy.wait()
    for copy in ring_copies.values():
        copy.wait_send()


VMEM, SMEM = pl.BlockSpec(memory_space=pltpu.VMEM), pl.BlockSpec(memory_space=pltpu.SMEM)
ANY = pl.BlockSpec(memory_space=pl.ANY)


def run_plan(keep, owner):
    return pl.pallas_call(
        plan,
        out_shape=(
            jax.ShapeDtypeStruct((2, SECOND), I32),
            jax.ShapeDtypeStruct((LANES,), I32),
            jax.ShapeDtypeStruct((BLOCKS,), I32),
            jax.ShapeDtypeStruct((NZ, 128), I32),
        ),
        in_specs=[SMEM] * 2,
        out_specs=(SMEM,) * 4,
        scratch_shapes=[pltpu.SMEM((NZ * LANES,), I32)],
        name="plan",
    )(keep, owner)


def run_exchange(slots, collective_id, scale2, operands):
    s1, s2, s3, s4 = slots
    block = (BLOCKS * 8, 128)

    def buffers(count):
        return (pltpu.VMEM((count, *block), BF16),) * 2

    return pl.pallas_call(
        functools.partial(exchange, slots, scale2),
        out_shape=(
            jax.ShapeDtypeStruct((HEADS, BLOCKS * BLOCK), F32),
            jax.ShapeDtypeStruct((STEP_ROWS, 128), BF16),
            jax.ShapeDtypeStruct((LANES, NZ, 1, 128), I32),
            jax.ShapeDtypeStruct((1, 128), I32),
            jax.ShapeDtypeStruct((NZ * LANES, *block), BF16),
            jax.ShapeDtypeStruct((NZ * LANES, *block), BF16),
        ),
        in_specs=[SMEM] * 4 + [VMEM] * 7,
        out_specs=(VMEM,) * 4 + (ANY,) * 2,
        scratch_shapes=[
            buffers(s1),
            buffers(s1),
            buffers(s1),
            buffers(s2),
            buffers(s3),
            buffers(s1),
            buffers(s2),
            buffers(s3),
            buffers(2 * s4),
            pltpu.VMEM((2, NZ, LANES, *block), BF16),
            pltpu.VMEM((BLOCKS * 256, 128), F32),
            pltpu.VMEM((HEADS * 8, 256, WINDOW * GROUP), BF16),
            pltpu.VMEM((HEADS * 8, WINDOW * GROUP), F32),
            pltpu.VMEM((HEADS * 8, WINDOW * GROUP), F32),
            pltpu.VMEM((HEADS * 8, 256), F32),
            pltpu.VMEM((8, STEP_ROWS, 1024), F32),
            pltpu.VMEM((HEADS, 16, WINDOW * GROUP), BF16),
            pltpu.VMEM((NZ, 1, 128), I32),
            pltpu.VMEM((2, 1, 128), I32),
            pltpu.SMEM((NZ, 1, 128), I32),
            pltpu.VMEM((LANES, 8, 768), F32),
            pltpu.VMEM((NZ, 8, 768), F32),
            pltpu.VMEM((LANES, STEP_ROWS + 8, 128), F32),
            pltpu.VMEM((NZ, STEP_ROWS + 8, 128), F32),
            pltpu.SemaphoreType.DMA((2, 2, 16)),
            pltpu.SemaphoreType.DMA((2, 2, 16)),
            pltpu.SemaphoreType.DMA((2, NZ, LANES)),
            pltpu.SemaphoreType.DMA((2, NZ, LANES)),
            pltpu.SemaphoreType.DMA((8, 8)),
            pltpu.SemaphoreType.DMA((8, 8)),
            pltpu.SemaphoreType.DMA,
        ],
        compiler_params=pltpu.CompilerParams(
            collective_id=collective_id,
            has_side_effects=True,
            vmem_limit_bytes=67_043_328,
        ),
        name="exchange_%d" % s1,
    )(*operands)


def unpack(meta, came_k, came_v, out_k, out_v, picks, sems):
    me_lane = lax.axis_index("ctx_1") * 2 + lax.axis_index("ctx_2")

    def choose(source, found):
        z, lane = source // LANES, lax.rem(source, LANES)
        picks[found] = source
        return found + (meta[lane * NZ + z, me_lane] > 0).astype(I32)

    lax.fori_loop(0, NZ * LANES, choose, 0)

    def copies(j):
        at = picks[j]
        return (
            pltpu.make_async_copy(came_k.at[at], out_k.at[j], sems.at[0, j]),
            pltpu.make_async_copy(came_v.at[at], out_v.at[j], sems.at[1, j]),
        )

    def start(j, carry):
        for copy in copies(j):
            copy.start()
        return carry

    def wait(j, carry):
        for copy in copies(j):
            copy.wait()
        return carry

    lax.fori_loop(0, KEEP, start, 0)
    lax.fori_loop(0, KEEP, wait, 0)


def run_unpack(meta, came_k, came_v):
    shape = jax.ShapeDtypeStruct((KEEP, *came_k.shape[1:]), BF16)
    return pl.pallas_call(
        unpack,
        out_shape=(shape, shape),
        in_specs=[SMEM, ANY, ANY],
        out_specs=(VMEM, VMEM),
        scratch_shapes=[
            pltpu.SMEM((NZ * LANES + 1,), I32),
            pltpu.SemaphoreType.DMA((2, KEEP)),
        ],
        name="unpack",
    )(meta.reshape(NZ * LANES, 128), came_k, came_v)


def shards(
    stored_keys,
    stored_values,
    observed_queries,
    decoded_queries,
    step_keys,
    decoded_values,
    keep_lists,
    owner_ids,
    cache_length,
):
    tokens, head_count, width = stored_keys.shape
    scale2 = math.log2(math.e) / math.sqrt(width)
    lists, own, kept, meta = run_plan(keep_lists, owner_ids)
    operands = (
        lists,
        own,
        kept,
        cache_length,
        meta.reshape(NZ, 1, 128),
        stored_keys.reshape(BLOCKS, BLOCK * head_count, width),
        stored_values.reshape(BLOCKS, BLOCK * head_count, width),
        observed_queries.transpose(1, 0, 2).reshape(HEADS, GROUP * WINDOW, width),
        decoded_queries.transpose(1, 0, 2).reshape(STEP_ROWS, width),
        step_keys.reshape(STEPS * HEADS, width),
        decoded_values.reshape(STEPS * HEADS, width),
    )
    scores, decoded, came, needs, came_k, came_v = run_exchange(FITS_MOST, 0, scale2, operands)
    fits = jnp.all(needs[0, LANES : LANES + 4] <= jnp.array(FITS_MOST, I32))

    def done():
        return run_unpack(came, came_k, came_v)

    def again():
        _, _, came, _, came_k, came_v = run_exchange(FITS_ALL, 1, scale2, operands)
        return run_unpack(came, came_k, came_v)

    kept_keys, kept_values = lax.cond(fits, done, again)
    decoded = decoded.reshape(HEAD_ROWS, STEPS, width).transpose(1, 0, 2)
    shape = (KEEP * BLOCK, head_count, width)
    return scores, kept_keys.reshape(shape), kept_values.reshape(shape), decoded


def solution(mesh):
    split = Mesh(
        mesh.devices.reshape(mesh.shape["batch"], 8, 4, 2, mesh.shape["head"]),
        ("batch", "ctx_0", "ctx_1", "ctx_2", "head"),
    )
    return jax.shard_map(
        shards,
        mesh=split,
        in_specs=(
            P(BATCH_CTX, "head", None),
            P(BATCH_CTX, "head", None),
            P("batch", "head", None),
            P("batch", "head", None),
            P("batch", "head", None),
            P("batch", "head", None),
            P(BATCH_CTX, None),
            P(BATCH_CTX, None),
            P("batch"),
        ),
        out_specs=(
            P(("batch", "head"), CTX),
            P(BATCH_CTX, "head", None),
            P(BATCH_CTX, "head", None),
            P("batch", "head", None),
        ),
        check_vma=False,
    )
```

time: 230 us -> 183 us (0.80)
  starting transfers between devices: 14.9 us -> 0 us
  local copies, waits for them, and re-layouts: 15.5 us -> 2.72 us
  between operations: 12.2 us -> 1.96 us
  other arithmetic: 11.6 us -> 1.37 us
  Pallas kernels: 166 us -> 176 us
  waiting for transfers between devices: 8.38 us -> 0 us
    all_to_all x1 -> x0, starting transfers between devices: 14.9 us -> none  [shards(): got = lax.all_to_all(row, BATCH_CTX, 0, 0, tiled=True)]
    pallas_call x1 -> x3, Pallas kernels: 166 us -> 176 us  [the longest x1 168 us: run_exchange(): pl.pallas_call(functools.partial(exchange, slots, scale2), out_shape=(jax...]
    all_to_all x1 -> x0, waiting for transfers between devices: 8.38 us -> none  [shards(): got = lax.all_to_all(row, BATCH_CTX, 0, 0, tiled=True)]
    another operation x9 -> x0, local copies, waits for them, and re-layouts: 3.18 us -> none
    select_n x8 -> x0, other arithmetic: 3 us -> none  [the longest x1 1.29 us: shards(): jnp.where(kept & (base + wide // head_count < seq), 0.0, FAR)]
    unnamed x5 -> x2, local copies, waits for them, and re-layouts: 5.35 us -> 2.72 us
    pad x2 -> x0, local copies, waits for them, and re-layouts: 2.61 us -> none  [padded(): return jnp.pad(flat, ((0, 128 - step_count * head_count), (0, 0)))]
  transfers between devices with their start and end apart: 1 -> 0, of which waited for: 1 -> 0; matrix products, arithmetic and copies ran while one was open for 1% -> 0% of each run, Pallas kernels for 0% -> 0%
where the time goes in v3:
time: 183 us; the launch traced here: 182 us
  Pallas kernels  176 us (96%)
  local copies, waits for them, and re-layouts  2.72 us (1%)
  between operations  1.96 us (1%)
    pallas_call x1, Pallas kernels, run_exchange(): pl.pallas_call(functools.partial(exchange, slots, scale2), out_shape=(jax...  168 us
    pallas_call x1, Pallas kernels, run_unpack(): pl.pallas_call(unpack, out_shape=(shape, shape), in_specs=[SMEM, ANY, ANY...  6.34 us

profile of v3, /device:TPU:1, one launch (start us, length us, event | category | flops | bytes accessed | tf_op | source)
XLA Modules:
  0.0 182.5 jit_solution(16388081254458955937)
XLA Ops:
  1.3 2.0 %plan.1 = (s32[2,32]{1,0:T(2,128)}, s32[8]{0:T(128)}, s32[32]{0:T(128)}, s32[8,128]{1,0:T(8,128)}) custom-call(s32[1,26]{1,0:T(1,128)} %keep.1, s32[1,26]{1,0:T(1,128)} %owner.1), custom_call_target="tpu_custom_call" | custom-call | tf_op jit(solution)/shard_map/plan/pallas_call | solution.py:521
  3.3 167.9 %exchange_17.1 = (f32[4,2048]{1,0:T(4,128)}, bf16[80,128]{1,0:T(8,128)(2,1)}, s32[8,8,1,128]{3,2,1,0:T(1,128)}, s32[1,128]{1,0:T(1,128)}, bf16[64,256,128]{2,1,0:T(8,128)(2,1)}, /*index=5*/bf16[64,256,128]{2,1,0:T(8,128)(2,1)}) custom-call(s32[2,32]{1,0:T(2,128)} %get-tuple-element.71.lists, s32[8]{0:T(128)} %get-tuple-element.72.own, ...), custom_call_target="tpu_custom_call" | custom-call | tf_op jit(solution)/shard_map/exchange_17/pallas_call | solution.py:543
  171.2 1.4 compare_reduce_fusion
  173.2 6.5 %conditional.1 = (bf16[1664,4,128]{2,1,0:T(4,128)(2,1)}, bf16[1664,4,128]{2,1,0:T(4,128)(2,1)}) conditional(s32[]{:T(128)} %convert_element_type.3, (s32[2,32]{1,0:T(2,128)}, s32[8]{0:T(128)}, s32[32]{0:T(128)}, s32[1]{0:T(128)}, s32[8,1,128]{2,1,0:T(1,128)}, /*index=5*/bf16[32,256,128]{2,1,0:T(8,128)(2,1)}, bf16[32,256,128]{2,1,0:T(8,128)(2,1)}, ...), branch_computations={%region_1.0_spmd, %region_2.0_spmd} | conditional | bytes 16 | solution.py:680
  173.4 6.3 %unpack.3 = (bf16[26,256,128]{2,1,0:T(8,128)(2,1)}, bf16[26,256,128]{2,1,0:T(8,128)(2,1)}) custom-call(s32[64,128]{1,0:T(8,128)} %bitcast.30, bf16[64,256,128]{2,1,0:T(8,128)(2,1)} %get-tuple-element.51.came_k, bf16[64,256,128]{2,1,0:T(8,128)(2,1)} %get-tuple-element.52.came_v), custom_call_target="tpu_custom_call" | custom-call | tf_op jit(solution)/shard_map/cond/branch_1_fun/unpack/pallas_call | solution.py:630
  179.8 1.4 copy.22
  181.1 1.3 copy.23

commit v4 on v3

--- a/solution.py
+++ b/solution.py
@@ -26,6 +26,7 @@
 STEP_ROWS = STEPS * HEAD_ROWS
 WINDOW = 128
 KEEP = 26
+PARTS = 4
 BLOCKS = 32
 SECOND = 32
 FITS_ALL = (26, 20, 12, 4)
@@ -110,8 +111,8 @@
     kept,
     length,
     meta,
-    keys,
-    values,
+    keys_in,
+    values_in,
     queries,
     step_queries,
     new_keys,
@@ -119,9 +120,12 @@
     out_scores,
     out_decoded,
     out_meta,
-    out_needs,
+    out_over,
     yr_k,
     yr_v,
+    keys,
+    values,
+    in_sem,
     zs_p,
     zs_m,
     zr_p1,
@@ -142,10 +146,14 @@
     meta_ring,
     needs_pair,
     table,
+    stat_out,
     stat_plane,
     stat_ring,
+    stat_all,
+    sum_out,
     sum_plane,
     sum_ring,
+    sum_all,
     z_send,
     z_recv,
     y_send,
@@ -158,8 +166,11 @@
     me_z = lax.axis_index("ctx_0")
     me_lane = lax.axis_index("ctx_1") * 2 + lax.axis_index("ctx_2")
     s1, s2, s3, s4 = slots
-    stores = (keys, values)
-    results = (yr_k, yr_v)
+    halves = PARTS // 2
+    rows_part = keys.shape[1] // halves
+
+    def part_of(pair, part):
+        return pair[part // halves], pl.ds(part % halves * rows_part, rows_part)
 
     def ring_peer(k):
         return {"ctx_0": lax.rem(me_z + (k + NZ), NZ)}
@@ -170,6 +181,13 @@
 
     def pair_peer(i):
         return {"batch": 1 - me_b}
+
+    loads = [
+        pltpu.make_async_copy(source, store, in_sem.at[kind])
+        for kind, (source, store) in enumerate(((keys_in, keys), (values_in, values)))
+    ]
+    for load in loads:
+        load.start()
 
     barrier = pltpu.get_barrier_semaphore()
     for i in range(1, LANES):
@@ -178,20 +196,25 @@
         pl.semaphore_signal(barrier, inc=1, device_id=ring_peer(k), device_id_type=MESH)
     pl.semaphore_signal(barrier, inc=1, device_id=pair_peer(0), device_id_type=MESH)
 
-    def pack_lists(slot, carry):
-        for way, dst in ((0, zs_p), (1, zs_m)):
-            at = lists[way, slot]
-            for kind in range(2):
-                dst[kind][slot] = stores[kind][at]
-        return carry
-
-    lax.fori_loop(0, s1, pack_lists, 0)
-    for i in range(LANES):
-        at = own[lax.rem(me_lane + i, LANES)]
-        for kind in range(2):
-            yb[kind, 0, i] = stores[kind][at]
+    def pack(part):
+        store, rows = part_of((keys, values), part)
+
+        def fill(slot, carry):
+            for way, dst in ((0, zs_p), (1, zs_m)):
+                dst[part][slot] = store[lists[way, slot], rows]
+            return carry
+
+        lax.fori_loop(0, s1, fill, 0)
+
+    def pack_own(part):
+        store, rows = part_of((keys, values), part)
+        for i in range(LANES):
+            yb[part, 0, i] = store[own[lax.rem(me_lane + i, LANES)], rows]
+
+    loads[0].wait()
+    for part in range(halves):
+        pack(part)
     meta_ring[me_z] = meta[me_z]
-
     pl.semaphore_wait(barrier, LANES - 1 + NZ - 1 + 1)
 
     def share(source, buffer, number, at, peer, count):
@@ -221,46 +244,46 @@
     ring = ((zs_p, zr_p1, zr_p2, zr_p3), (zs_m, zr_m1, zr_m2, zr_m3))
     ring_copies = {}
 
-    def ring_start(kind, way, q, hop):
+    def ring_start(part, way, q, hop):
         a, b = segments[q]
         if a == b:
             return
-        src = ring[way][hop - 1][kind].at[pl.ds(a, b - a)]
+        src = ring[way][hop - 1][part].at[pl.ds(a, b - a)]
         if hop < HALF:
-            dst = ring[way][hop][kind].at[pl.ds(a, b - a)]
+            dst = ring[way][hop][part].at[pl.ds(a, b - a)]
         else:
-            dst = zr_4[kind].at[pl.ds(way * s4 + a, b - a)]
+            dst = zr_4[part].at[pl.ds(way * s4 + a, b - a)]
         number = q * HALF + hop - 1
         copy = pltpu.make_async_remote_copy(
             src_ref=src,
             dst_ref=dst,
-            send_sem=z_send.at[kind, way, number],
-            recv_sem=z_recv.at[kind, way, number],
+            send_sem=z_send.at[part, way, number],
+            recv_sem=z_recv.at[part, way, number],
             device_id=ring_peer(1 if way == 0 else -1),
             device_id_type=MESH,
         )
         copy.start()
-        ring_copies[kind, way, q, hop] = copy
-
-    def arrived(kind, q, hop):
+        ring_copies[part, way, q, hop] = copy
+
+    def arrived(part, q, hop):
         for way in range(2):
-            if (kind, way, q, hop) in ring_copies:
-                ring_copies[kind, way, q, hop].wait_recv()
-
-    def hand_on(kind, hop):
+            if (part, way, q, hop) in ring_copies:
+                ring_copies[part, way, q, hop].wait_recv()
+
+    def hand_on(part, hop):
         for q in range(HALF - hop):
             for way in range(2):
-                if (kind, way, q, hop) in ring_copies:
-                    ring_copies[kind, way, q, hop].wait_recv()
-                ring_start(kind, way, q, hop + 1)
-        arrived(kind, HALF - hop, hop)
+                if (part, way, q, hop) in ring_copies:
+                    ring_copies[part, way, q, hop].wait_recv()
+                ring_start(part, way, q, hop + 1)
+        arrived(part, HALF - hop, hop)
 
     arrivals = {1: zr_p1, 2: zr_p2, 3: zr_p3, 4: zr_4, 5: zr_m3, 6: zr_m2, 7: zr_m1}
     plane_copies = {}
 
-    def plane_pack(kind, b):
+    def plane_pack(part, b):
         source = lax.rem(me_z + (NZ - b), NZ)
-        got = arrivals[b][kind]
+        got = arrivals[b][part]
         for i in range(LANES):
             code = table[source, 0, lax.rem(me_lane + i, LANES)]
             is_second = (code > SECOND).astype(I32)
@@ -269,39 +292,51 @@
                 slot = lax.min(slot, s4 - 1) + is_second * s4
             else:
                 slot = lax.min(slot, got.shape[0] - 1)
-            yb[kind, b, i] = got[slot]
-
-    def plane_start(kind, b):
+            yb[part, b, i] = got[slot]
+
+    def plane_start(part, b):
+        result, rows = part_of((yr_k, yr_v), part)
         source = lax.rem(me_z + (NZ - b), NZ) * LANES + me_lane
         for i in range(1, LANES):
             copy = pltpu.make_async_remote_copy(
-                src_ref=yb.at[kind, b, i],
-                dst_ref=results[kind].at[source],
-                send_sem=y_send.at[kind, b, i],
-                recv_sem=y_recv.at[kind, b, i],
+                src_ref=yb.at[part, b, i],
+                dst_ref=result.at[source, rows],
+                send_sem=y_send.at[part, b, i],
+                recv_sem=y_recv.at[part, b, i],
                 device_id=plane_peer(i),
                 device_id_type=MESH,
             )
             copy.start()
-            plane_copies[kind, b, i] = copy
+            plane_copies[part, b, i] = copy
         copy = pltpu.make_async_copy(
-            yb.at[kind, b, 0], results[kind].at[source], y_send.at[kind, b, 0]
+            yb.at[part, b, 0], result.at[source, rows], y_send.at[part, b, 0]
         )
         copy.start()
-        plane_copies[kind, b, 0] = copy
-
-    def across(kind, *batches):
+        plane_copies[part, b, 0] = copy
+
+    def across(part, *batches):
         for b in batches:
-            plane_pack(kind, b)
+            plane_pack(part, b)
         for b in batches:
-            plane_start(kind, b)
-
-    for kind in range(2):
-        for q in range(HALF):
+            plane_start(part, b)
+
+    def ring_first(part, *parts):
+        for q in parts:
             for way in range(2):
-                ring_start(kind, way, q, 1)
-    plane_start(0, 0)
-    plane_start(1, 0)
+                ring_start(part, way, q, 1)
+
+    every = range(HALF)
+    for part in range(halves):
+        ring_first(part, *every)
+    loads[1].wait()
+    for part in range(halves, PARTS):
+        pack(part)
+    for part in range(halves, PARTS - 1):
+        ring_first(part, *every)
+    for part in range(PARTS):
+        pack_own(part)
+    for part in range(PARTS):
+        plane_start(part, 0)
 
     def widen(c, carry):
         kf[pl.ds(pl.multiple_of(c * 256, 256), 256), :] = keys[c].astype(F32)
@@ -387,37 +422,46 @@
                 keepdims=True,
             )
         )
-    stat_plane[me_lane, :, :640] = jnp.concatenate(maxima + sums, axis=0)
-    stat_plane[me_lane, :, 640:] = jnp.broadcast_to(step_top, (8, 128))
+    tiles = [
+        tuple(found[g][:, t * 128 : (t + 1) * 128] for found in (maxima, sums))
+        for g in range(HEADS)
+        for t in range(GROUP)
+    ] + [(step_top, jnp.zeros((1, 128), F32))]
+    stat_out[...] = jnp.zeros_like(stat_out)
+    for n, (tile_max, tile_sum) in enumerate(tiles):
+        stat_out[n // 3, n % 3 : n % 3 + 1, :] = tile_max
+        stat_out[n // 3, n % 3 + 3 : n % 3 + 4, :] = tile_sum
+    stat_plane[me_lane] = stat_out[me_lane]
+
+    def plane_slice(buffer):
+        return lambda i: buffer.at[lax.rem(me_lane + i, LANES)]
 
     settle(metas)
     to_scalars = pltpu.make_async_copy(meta_ring, table, t_sem)
     to_scalars.start()
     to_scalars.wait()
     out_meta[me_lane] = meta_ring[...]
-    stats = share(lambda i: stat_plane.at[me_lane], stat_plane, 0, me_lane, plane_peer, LANES)
+    stats = share(plane_slice(stat_out), stat_plane, 0, me_lane, plane_peer, LANES)
     metas = share(lambda i: meta_ring, out_meta, 5, me_lane, plane_peer, LANES)
 
-    def merged(buffer, count):
-        largest = buffer[0, :4, :640]
-        step_max = buffer[0, :, 640:]
-        for k in range(1, count):
-            largest = jnp.maximum(largest, buffer[k, :4, :640])
-            step_max = jnp.maximum(step_max, buffer[k, :, 640:])
-        total = jnp.zeros((4, 640), F32)
-        for k in range(count):
-            total = total + buffer[k, 4:, :640] * jnp.exp2(
-                (buffer[k, :4, :640] - largest) * scale2
-            )
-        return largest, total, step_max
+    def merged(buffer):
+        largest = buffer[0, 0:3, :]
+        for k in range(1, 8):
+            largest = jnp.maximum(largest, buffer[k, 0:3, :])
+        total = jnp.zeros((3, 128), F32)
+        for k in range(8):
+            total = total + buffer[k, 3:6, :] * jnp.exp2((buffer[k, 0:3, :] - largest) * scale2)
+        return largest, total
 
     settle(stats)
-    largest, total, step_max = merged(stat_plane, LANES)
-    stat_ring[me_z, :, :640] = jnp.concatenate([largest, total], axis=0)
-    stat_ring[me_z, :, 640:] = step_max
+    largest, total = merged(stat_plane)
+    stat_ring[me_z, 0:3, :] = largest
+    stat_ring[me_z, 3:6, :] = total
     stats = share(lambda k: stat_ring.at[me_z], stat_ring, 1, me_z, ring_peer, NZ)
-    hand_on(0, 1)
-    across(0, 1, 7)
+    ring_first(PARTS - 1, *every)
+    for part in range(PARTS):
+        hand_on(part, 1)
+        across(part, 1, 7)
     settle(metas)
     most = out_meta[0, 0]
     for lane in range(LANES):
@@ -425,12 +469,27 @@
             most = jnp.maximum(most, out_meta[lane, z])
     needs_pair[me_b] = most
     pair = share(lambda i: needs_pair.at[me_b], needs_pair, 6, me_b, pair_peer, 2)
-    hand_on(1, 1)
-    across(1, 1, 7)
 
     settle(stats)
-    row_max, row_total, step_max = merged(stat_ring, NZ)
-    step_column = row_to_column(step_max[:1, :], STEP_ROWS)
+    largest, total = merged(stat_ring)
+    stat_all[me_lane, 0:3, :] = largest
+    stat_all[me_lane, 3:6, :] = total
+    stats = share(lambda i: stat_all.at[me_lane], stat_all, 7, me_lane, plane_peer, LANES)
+    for part in range(PARTS // 2):
+        hand_on(part, 2)
+        across(part, 2, 6)
+
+    settle(stats)
+
+    def across_tiles(first, g):
+        tiles = range(g * GROUP, (g + 1) * GROUP)
+        return jnp.concatenate(
+            [stat_all[n // 3, first + n % 3 : first + n % 3 + 1, :] for n in tiles], axis=1
+        )
+
+    row_max = [across_tiles(0, g) for g in range(HEADS)]
+    row_total = [across_tiles(3, g) for g in range(HEADS)]
+    step_column = row_to_column(stat_all[6, 2:3, :], STEP_ROWS)
 
     def decode_sum(c, carry):
         weighted, total = carry
@@ -443,26 +502,18 @@
 
     nothing = jnp.zeros((STEP_ROWS, 128), F32)
     weighted, total = lax.fori_loop(0, 8, decode_sum, (nothing, nothing))
-    sum_plane[me_lane, :STEP_ROWS, :] = weighted
-    sum_plane[me_lane, STEP_ROWS:, :] = jnp.broadcast_to(
-        column_to_row(jnp.sum(total, axis=1, keepdims=True)), (8, 128)
-    )
-    sums = share(lambda i: sum_plane.at[me_lane], sum_plane, 2, me_lane, plane_peer, LANES)
-    hand_on(0, 2)
-    across(0, 2, 6)
-    settle(sums)
-    total = sum_plane[0]
-    for k in range(1, LANES):
-        total = total + sum_plane[k]
-    sum_ring[me_z] = total
-    sums = share(lambda k: sum_ring.at[me_z], sum_ring, 3, me_z, ring_peer, NZ)
-    hand_on(1, 2)
-    across(1, 2, 6)
+    bottom = column_to_row(jnp.sum(total, axis=1, keepdims=True))
+    each = STEP_ROWS // LANES
+    for lane in range(LANES):
+        sum_out[lane, 0:each, :] = weighted[lane * each : (lane + 1) * each]
+        sum_out[lane, each:16, :] = jnp.broadcast_to(bottom, (16 - each, 128))
+    sum_plane[me_lane] = sum_out[me_lane]
+    sums = share(plane_slice(sum_out), sum_plane, 2, me_lane, plane_peer, LANES)
 
     for g in range(HEADS):
         factor = (
-            jnp.exp2((chunk_max[g * 8 : g * 8 + 8, :] - row_max[g : g + 1]) * scale2)
-            / row_total[g : g + 1]
+            jnp.exp2((chunk_max[g * 8 : g * 8 + 8, :] - row_max[g]) * scale2)
+            / row_total[g]
         )
         high = factor.astype(BF16)
         low = (factor - high.astype(F32)).astype(BF16)
@@ -479,35 +530,53 @@
         redundancy[pl.ds(i, 1), :] = jnp.where(live, value, 0.0)
         return carry
 
-    lax.fori_loop(0, HEADS * 8, importance, 0)
+    for part in range(PARTS // 2, PARTS):
+        hand_on(part, 2)
+        across(part, 2, 6)
+        piece = part - PARTS // 2
+        lax.fori_loop(piece * 64 // PARTS, (piece + 1) * 64 // PARTS, importance, 0)
+
+    def summed(buffer):
+        total = buffer[0]
+        for k in range(1, 8):
+            total = total + buffer[k]
+        return total
+
+    settle(sums)
+    sum_ring[me_z] = summed(sum_plane)
+    sums = share(lambda k: sum_ring.at[me_z], sum_ring, 3, me_z, ring_peer, NZ)
+    for part in range(PARTS):
+        hand_on(part, 3)
+        across(part, 3, 5)
+    settle(sums)
+    sum_all[me_lane] = summed(sum_ring)
+    sums = share(lambda i: sum_all.at[me_lane], sum_all, 8, me_lane, plane_peer, LANES)
     for g in range(HEADS):
         for c in range(8):
             out_scores[g : g + 1, c * 256 : (c + 1) * 256] = redundancy[g * 8 + c : g * 8 + c + 1, :]
     settle(pair)
-    out_needs[...] = jnp.maximum(needs_pair[0], needs_pair[1])
-
-    hand_on(0, 3)
-    across(0, 3, 5)
-    hand_on(1, 3)
-    across(1, 3, 5)
+    over = jnp.maximum(needs_pair[0], needs_pair[1])
+    lane = lax.broadcasted_iota(I32, (1, 128), 1)
+    for n in range(4):
+        over = jnp.where(lane == LANES + n, over - slots[n], over)
+    over = jnp.where((lane >= LANES) & (lane < LANES + 4), over, -1)
+    out_over[0] = jnp.max(over)
+
+    for part in range(PARTS):
+        arrived(part, 0, HALF)
+        across(part, HALF)
 
     settle(sums)
-    total = sum_ring[0]
-    for k in range(1, NZ):
-        total = total + sum_ring[k]
     fresh = jnp.exp2((new_logits - step_column) * scale2)
-    weighted = total[:STEP_ROWS] + jnp.dot(
+    weighted = jnp.concatenate([sum_all[lane, 0:each, :] for lane in range(LANES)], axis=0)
+    weighted = weighted + jnp.dot(
         fresh.astype(BF16), padded(new_values), preferred_element_type=F32
     )
-    bottom = row_to_column(total[STEP_ROWS : STEP_ROWS + 1, :], STEP_ROWS)
+    bottom = row_to_column(sum_all[0, each : each + 1, :], STEP_ROWS)
     bottom = bottom + jnp.sum(fresh, axis=1, keepdims=True)
     out_decoded[...] = (weighted / bottom).astype(BF16)
 
-    for kind in range(2):
-        arrived(kind, 0, HALF)
-        across(kind, HALF)
-
-    for (kind, b, i), copy in plane_copies.items():
+    for (part, b, i), copy in plane_copies.items():
         copy.wait()
     for copy in ring_copies.values():
         copy.wait_send()
@@ -537,8 +606,10 @@
     s1, s2, s3, s4 = slots
     block = (BLOCKS * 8, 128)
 
+    slot = (block[0] * 2 // PARTS, 128)
+
     def buffers(count):
-        return (pltpu.VMEM((count, *block), BF16),) * 2
+        return (pltpu.VMEM((count, *slot), BF16),) * PARTS
 
     return pl.pallas_call(
         functools.partial(exchange, slots, scale2),
@@ -546,13 +617,16 @@
             jax.ShapeDtypeStruct((HEADS, BLOCKS * BLOCK), F32),
             jax.ShapeDtypeStruct((STEP_ROWS, 128), BF16),
             jax.ShapeDtypeStruct((LANES, NZ, 1, 128), I32),
-            jax.ShapeDtypeStruct((1, 128), I32),
+            jax.ShapeDtypeStruct((1,), I32),
             jax.ShapeDtypeStruct((NZ * LANES, *block), BF16),
             jax.ShapeDtypeStruct((NZ * LANES, *block), BF16),
         ),
-        in_specs=[SMEM] * 4 + [VMEM] * 7,
-        out_specs=(VMEM,) * 4 + (ANY,) * 2,
+        in_specs=[SMEM] * 4 + [VMEM, ANY, ANY] + [VMEM] * 4,
+        out_specs=(VMEM,) * 3 + (SMEM,) + (ANY,) * 2,
         scratch_shapes=[
+            pltpu.VMEM((BLOCKS, *block), BF16),
+            pltpu.VMEM((BLOCKS, *block), BF16),
+            pltpu.SemaphoreType.DMA((2,)),
             buffers(s1),
             buffers(s1),
             buffers(s1),
@@ -562,7 +636,7 @@
             buffers(s2),
             buffers(s3),
             buffers(2 * s4),
-            pltpu.VMEM((2, NZ, LANES, *block), BF16),
+            pltpu.VMEM((PARTS, NZ, LANES, *slot), BF16),
             pltpu.VMEM((BLOCKS * 256, 128), F32),
             pltpu.VMEM((HEADS * 8, 256, WINDOW * GROUP), BF16),
             pltpu.VMEM((HEADS * 8, WINDOW * GROUP), F32),
@@ -573,16 +647,14 @@
             pltpu.VMEM((NZ, 1, 128), I32),
             pltpu.VMEM((2, 1, 128), I32),
             pltpu.SMEM((NZ, 1, 128), I32),
-            pltpu.VMEM((LANES, 8, 768), F32),
-            pltpu.VMEM((NZ, 8, 768), F32),
-            pltpu.VMEM((LANES, STEP_ROWS + 8, 128), F32),
-            pltpu.VMEM((NZ, STEP_ROWS + 8, 128), F32),
-            pltpu.SemaphoreType.DMA((2, 2, 16)),
-            pltpu.SemaphoreType.DMA((2, 2, 16)),
-            pltpu.SemaphoreType.DMA((2, NZ, LANES)),
-            pltpu.SemaphoreType.DMA((2, NZ, LANES)),
-            pltpu.SemaphoreType.DMA((8, 8)),
-            pltpu.SemaphoreType.DMA((8, 8)),
+            *[pltpu.VMEM((8, 8, 128), F32)] * 4,
+            *[pltpu.VMEM((8, 16, 128), F32)] * 4,
+            pltpu.SemaphoreType.DMA((PARTS, 2, 16)),
+            pltpu.SemaphoreType.DMA((PARTS, 2, 16)),
+            pltpu.SemaphoreType.DMA((PARTS, NZ, LANES)),
+            pltpu.SemaphoreType.DMA((PARTS, NZ, LANES)),
+            pltpu.SemaphoreType.DMA((10, 8)),
+            pltpu.SemaphoreType.DMA((10, 8)),
             pltpu.SemaphoreType.DMA,
         ],
         compiler_params=pltpu.CompilerParams(
@@ -594,7 +666,9 @@
     )(*operands)
 
 
-def unpack(meta, came_k, came_v, out_k, out_v, picks, sems):
+def unpack(
+    meta, scores, decoded, came_k, came_v, out_scores, out_decoded, out_k, out_v, held, picks, sems
+):
     me_lane = lax.axis_index("ctx_1") * 2 + lax.axis_index("ctx_2")
 
     def choose(source, found):
@@ -603,41 +677,58 @@
         return found + (meta[lane * NZ + z, me_lane] > 0).astype(I32)
 
     lax.fori_loop(0, NZ * LANES, choose, 0)
-
-    def copies(j):
-        at = picks[j]
-        return (
-            pltpu.make_async_copy(came_k.at[at], out_k.at[j], sems.at[0, j]),
-            pltpu.make_async_copy(came_v.at[at], out_v.at[j], sems.at[1, j]),
+    pairs = ((came_k, out_k), (came_v, out_v))
+
+    def take(kind, j):
+        return pltpu.make_async_copy(
+            pairs[kind][0].at[picks[j]], held.at[kind, j], sems.at[0, kind, j]
         )
 
-    def start(j, carry):
-        for copy in copies(j):
-            copy.start()
-        return carry
-
-    def wait(j, carry):
-        for copy in copies(j):
-            copy.wait()
-        return carry
-
-    lax.fori_loop(0, KEEP, start, 0)
-    lax.fori_loop(0, KEEP, wait, 0)
-
-
-def run_unpack(meta, came_k, came_v):
-    shape = jax.ShapeDtypeStruct((KEEP, *came_k.shape[1:]), BF16)
+    def put(kind, j):
+        return pltpu.make_async_copy(held.at[kind, j], pairs[kind][1].at[j], sems.at[1, kind, j])
+
+    for kind in range(2):
+
+        @pl.loop(0, KEEP)
+        def _(j, kind=kind):
+            take(kind, j).start()
+
+    out_scores[...] = scores[...]
+    out_decoded[...] = decoded[...]
+    for kind in range(2):
+
+        @pl.loop(0, KEEP)
+        def _(j, kind=kind):
+            take(kind, j).wait()
+            put(kind, j).start()
+
+    for kind in range(2):
+
+        @pl.loop(0, KEEP)
+        def _(j, kind=kind):
+            put(kind, j).wait()
+
+
+def run_unpack(meta, scores, decoded, came_k, came_v):
+    block = came_k.shape[1:]
+    shape = jax.ShapeDtypeStruct((KEEP, *block), BF16)
     return pl.pallas_call(
         unpack,
-        out_shape=(shape, shape),
-        in_specs=[SMEM, ANY, ANY],
-        out_specs=(VMEM, VMEM),
+        out_shape=(
+            jax.ShapeDtypeStruct(scores.shape, scores.dtype),
+            jax.ShapeDtypeStruct(decoded.shape, decoded.dtype),
+            shape,
+            shape,
+        ),
+        in_specs=[SMEM, VMEM, VMEM, ANY, ANY],
+        out_specs=(VMEM, VMEM, ANY, ANY),
         scratch_shapes=[
+            pltpu.VMEM((2, KEEP, *block), BF16),
             pltpu.SMEM((NZ * LANES + 1,), I32),
-            pltpu.SemaphoreType.DMA((2, KEEP)),
+            pltpu.SemaphoreType.DMA((2, 2, KEEP)),
         ],
         name="unpack",
-    )(meta.reshape(NZ * LANES, 128), came_k, came_v)
+    )(meta.reshape(NZ * LANES, 128), scores, decoded, came_k, came_v)
 
 
 def shards(
@@ -667,17 +758,17 @@
         step_keys.reshape(STEPS * HEADS, width),
         decoded_values.reshape(STEPS * HEADS, width),
     )
-    scores, decoded, came, needs, came_k, came_v = run_exchange(FITS_MOST, 0, scale2, operands)
-    fits = jnp.all(needs[0, LANES : LANES + 4] <= jnp.array(FITS_MOST, I32))
-
-    def done():
-        return run_unpack(came, came_k, came_v)
-
-    def again():
-        _, _, came, _, came_k, came_v = run_exchange(FITS_ALL, 1, scale2, operands)
-        return run_unpack(came, came_k, came_v)
-
-    kept_keys, kept_values = lax.cond(fits, done, again)
+    first = run_exchange(FITS_MOST, 0, scale2, operands)
+
+    def finish(result):
+        scores, decoded, came, _, came_k, came_v = result
+        return run_unpack(came, scores, decoded, came_k, came_v)
+
+    scores, decoded, kept_keys, kept_values = lax.cond(
+        first[3][0] > 0,
+        lambda: finish(run_exchange(FITS_ALL, 1, scale2, operands)),
+        lambda: finish(first),
+    )
     decoded = decoded.reshape(HEAD_ROWS, STEPS, width).transpose(1, 0, 2)
     shape = (KEEP * BLOCK, head_count, width)
     return scores, kept_keys.reshape(shape), kept_values.reshape(shape), decoded

time: 183 us -> 166 us (0.907)
  Pallas kernels: 176 us -> 163 us
  local copies, waits for them, and re-layouts: 2.72 us -> 0 us
    pallas_call x1, Pallas kernels: 168 us -> 154 us  [run_exchange(): pl.pallas_call(functools.partial(exchange, slots, scale2), out_shape=(jax...]
    unnamed x2 -> x0, local copies, waits for them, and re-layouts: 2.72 us -> none
where the time goes in v4:
time: 166 us; the launch traced here: 165 us
  Pallas kernels  163 us (98%)
  between operations  2.08 us (1%)
    pallas_call x1, Pallas kernels, run_exchange(): pl.pallas_call(functools.partial(exchange, slots, scale2), out_shape=(jax...  154 us
    pallas_call x1, Pallas kernels, run_unpack(): pl.pallas_call(unpack, out_shape=(jax.ShapeDtypeStruct(scores.shape, scor...  6.96 us

profile of v4, /device:TPU:1, one launch (start us, length us, event | category | flops | bytes accessed | tf_op | source)
XLA Modules:
  0.0 165.3 jit_solution(15129943733196618268)
XLA Ops:
  1.3 2.0 %plan.1 = (s32[2,32]{1,0:T(2,128)}, s32[8]{0:T(128)}, s32[32]{0:T(128)}, s32[8,128]{1,0:T(8,128)}) custom-call(s32[1,26]{1,0:T(1,128)} %keep.1, s32[1,26]{1,0:T(1,128)} %owner.1), custom_call_target="tpu_custom_call" | custom-call | tf_op jit(solution)/shard_map/plan/pallas_call | solution.py:590
  3.3 154.0 %exchange_17.1 = (f32[4,2048]{1,0:T(4,128)}, bf16[80,128]{1,0:T(8,128)(2,1)}, s32[8,8,1,128]{3,2,1,0:T(1,128)}, s32[1]{0:T(128)}, bf16[64,256,128]{2,1,0:T(8,128)(2,1)}, /*index=5*/bf16[64,256,128]{2,1,0:T(8,128)(2,1)}) custom-call(s32[2,32]{1,0:T(2,128)} %get-tuple-element.90.lists, s32[8]{0:T(128)} %get-tuple-element.91.own, s32[32]{0:T(128)} %get-tuple-element.92.kept, ...), custom_call_target="tpu_custom_call" | custom-call | tf_op jit(solution)/shard_map/exchange_17/pallas_call | solution.py:614
  157.9 7.2 %conditional.1 = ((f32[4,2048]{1,0:T(4,128)}, bf16[80,128]{1,0:T(8,128)(2,1)}, bf16[26,256,128]{2,1,0:T(8,128)(2,1)}, bf16[26,256,128]{2,1,0:T(8,128)(2,1)})) conditional(s32[]{:T(128)} %bitcast.13, (s32[8,8,1,128]{3,2,1,0:T(1,128)}, f32[4,2048]{1,0:T(4,128)}, bf16[80,128]{1,0:T(8,128)(2,1)}, bf16[64,256,128]{2,1,0:T(8,128)(2,1)}, ...), branch_computations={%region_0.0_spmd.clone, %region_1.0_spmd.clone} | conditional | bytes 8 | solution.py:767
  158.0 7.0 %unpack.4 = (f32[4,2048]{1,0:T(4,128)}, bf16[80,128]{1,0:T(8,128)(2,1)}, bf16[26,256,128]{2,1,0:T(8,128)(2,1)}, bf16[26,256,128]{2,1,0:T(8,128)(2,1)}) custom-call(s32[64,128]{1,0:T(8,128)} %bitcast.31, f32[4,2048]{1,0:T(4,128)} %get-tuple-element.126.scores, bf16[80,128]{1,0:T(8,128)(2,1)} %get-tuple-element.127.decoded, ...), custom_call_target="tpu_custom_call" | custom-call | tf_op jit(solution)/shard_map/cond/branch_0_fun/unpack/pallas_call | solution.py:715

commit v5 on v4

--- a/solution.py
+++ b/solution.py
@@ -50,67 +50,77 @@
     return jnp.transpose(wide)[:1, :]
 
 
-def plan(keep, owner, lists, own, kept, meta, block_of):
-    me_z = lax.axis_index("ctx_0")
-    for o in range(NZ * LANES):
-        block_of[o] = -1
-    for b in range(BLOCKS):
-        kept[b] = 0
-    for slot in range(SECOND):
-        lists[0, slot] = 0
-        lists[1, slot] = 0
-
-    def place(j, carry):
-        block_of[owner[0, j]] = keep[0, j]
-        kept[keep[0, j]] = 1
-        return carry
-
-    lax.fori_loop(0, KEEP, place, 0)
-    planes = [lax.rem(me_z + k, NZ) for k in range(NZ)]
-    blocks = [[block_of[planes[k] * LANES + i] for i in range(LANES)] for k in range(NZ)]
-    has = [[(b >= 0).astype(I32) for b in row] for row in blocks]
-    count = [sum(row[1:], row[0]) for row in has]
+def before_64(block):
+    row = lax.broadcasted_iota(I32, (64, 64), 0)
+    column = lax.broadcasted_iota(I32, (64, 64), 1)
+    return jnp.where((column < row) & (column // block == row // block), 1.0, 0.0).astype(BF16)
+
+
+def spread_rows(block):
+    shape = block.shape
+    same = lax.broadcasted_iota(I32, shape, 0) == lax.broadcasted_iota(I32, shape, 1)
+    return jnp.sum(jnp.where(same, block, 0.0), axis=0, keepdims=True)
+
+
+def plan(keep, owner, me_z, meta, lists):
+    ahead_of_me = (owner + (NZ - me_z) * LANES) & (NZ * LANES - 1)
+    match = lax.broadcasted_iota(I32, (NZ * LANES, KEEP), 0) == ahead_of_me
+    wide = (NZ * LANES, 128)
+    has = jnp.sum(jnp.where(match, 1.0, 0.0), axis=1, keepdims=True)
+    has = jnp.broadcast_to(has, wide)
+    block = jnp.sum(jnp.where(match, keep.astype(F32), 0.0), axis=1, keepdims=True)
+    block = jnp.broadcast_to(block, wide)
+    rank = jnp.dot(before_64(LANES), has.astype(BF16), preferred_element_type=F32)
+
+    def plane(values, k):
+        return values[k * LANES : (k + 1) * LANES]
+
+    count = [jnp.sum(plane(has, k), axis=0, keepdims=True) for k in range(NZ)]
     n4 = count[HALF]
     ahead, behind = count[1] + count[2] + count[3], count[7] + count[6] + count[5]
-    first = lax.max(n4 - 4, lax.min(lax.min(n4, 4), lax.max(0, (n4 + behind - ahead + 1) >> 1)))
-    first = lax.max(first, 0)
+    even = jnp.maximum(jnp.floor((n4 + behind - ahead + 1.0) * 0.5), 0.0)
+    first = jnp.maximum(jnp.maximum(n4 - 4.0, 0.0), jnp.minimum(jnp.minimum(n4, 4.0), even))
     second = n4 - first
     tails_p = [first, first + count[3], first + count[3] + count[2], first + ahead]
     tails_m = [second, second + count[5], second + count[5] + count[6], second + behind]
-    start = [0, tails_p[2], tails_p[1], tails_p[0], 0, tails_m[0], tails_m[1], tails_m[2]]
-    needs = [lax.max(p, m) for p, m in zip(tails_p[::-1], tails_m[::-1])]
+    none = jnp.zeros_like(first)
+    start = [none, tails_p[2], tails_p[1], tails_p[0], none, tails_m[0], tails_m[1], tails_m[2]]
+    needs = [jnp.maximum(p, m) for p, m in zip(tails_p[::-1], tails_m[::-1])]
+    lane = lax.broadcasted_iota(I32, (1, 128), 1)
+    ways, places = [], []
     for k in range(NZ):
-        rank = start[k] + jnp.zeros((), I32)
-        for i in range(LANES):
-            if k == HALF:
-                way = (rank >= first).astype(I32)
-                slot = rank - way * first
-            else:
-                way = jnp.full((), int(k > HALF), I32)
-                slot = rank
-            there = has[k][i]
-            meta[planes[k], i] = there * (slot + 1 + way * SECOND)
-            if k == 0:
-                own[i] = lax.max(blocks[k][i], 0)
-            else:
-
-                @pl.when(there > 0)
-                def _(way=way, slot=slot, block=blocks[k][i]):
-                    lists[way, slot] = block
-
-            rank = rank + there
+        if k == HALF:
+            way = jnp.where(plane(rank, k) >= first, 1.0, 0.0)
+        else:
+            way = jnp.full((LANES, 128), float(k > HALF), F32)
+        place = plane(rank, k) + start[k] - (way * first if k == HALF else 0.0)
+        row = spread_rows(plane(has, k) * (place + 1.0 + way * SECOND))
         for n in range(4):
-            meta[k, LANES + n] = needs[n]
+            row = jnp.where(lane == LANES + n, needs[n], row)
+        meta[lax.rem(me_z + k, NZ)] = row.astype(I32)
+        ways.append(way)
+        places.append(place)
+    way, place = jnp.concatenate(ways, axis=0), jnp.concatenate(places, axis=0)
+    slot = lax.broadcasted_iota(I32, wide, 1).astype(F32)
+    travels = (has > 0.5) & (lax.broadcasted_iota(I32, wide, 0) >= LANES)
+    fills = travels & (jnp.abs(place - slot) < 0.5)
+    for w in range(2):
+        chosen = fills & (jnp.abs(way - w) < 0.5)
+        row = jnp.sum(jnp.where(chosen, block, 0.0), axis=0, keepdims=True)
+        lists[w : w + 1, :] = row.astype(I32)
+    lists[2:3, :] = spread_rows(plane(block, 0)).astype(I32)
+    named = lax.broadcasted_iota(I32, (BLOCKS, KEEP), 0) == keep
+    named = jnp.sum(jnp.where(named, 1.0, 0.0), axis=1, keepdims=True)
+    lists[3:4, :] = spread_rows(jnp.broadcast_to(named, (BLOCKS, 128))).astype(I32)
+    lists[4:8, :] = jnp.zeros((4, 128), I32)
 
 
 def exchange(
     slots,
     scale2,
-    lists,
-    own,
-    kept,
     length,
-    meta,
+    keep,
+    owner,
     keys_in,
     values_in,
     queries,
@@ -119,13 +129,16 @@
     new_values,
     out_scores,
     out_decoded,
-    out_meta,
+    out_picks,
     out_over,
     yr_k,
     yr_v,
     keys,
     values,
     in_sem,
+    meta,
+    plan_rows,
+    planned,
     zs_p,
     zs_m,
     zr_p1,
@@ -144,6 +157,7 @@
     dl,
     rescale,
     meta_ring,
+    meta_all,
     needs_pair,
     table,
     stat_out,
@@ -196,12 +210,15 @@
         pl.semaphore_signal(barrier, inc=1, device_id=ring_peer(k), device_id_type=MESH)
     pl.semaphore_signal(barrier, inc=1, device_id=pair_peer(0), device_id_type=MESH)
 
+    def block_at(row, slot):
+        return lax.max(lax.min(planned[row, slot], BLOCKS - 1), 0)
+
     def pack(part):
         store, rows = part_of((keys, values), part)
 
         def fill(slot, carry):
             for way, dst in ((0, zs_p), (1, zs_m)):
-                dst[part][slot] = store[lists[way, slot], rows]
+                dst[part][slot] = store[block_at(way, slot), rows]
             return carry
 
         lax.fori_loop(0, s1, fill, 0)
@@ -209,8 +226,12 @@
     def pack_own(part):
         store, rows = part_of((keys, values), part)
         for i in range(LANES):
-            yb[part, 0, i] = store[own[lax.rem(me_lane + i, LANES)], rows]
-
+            yb[part, 0, i] = store[block_at(2, lax.rem(me_lane + i, LANES)), rows]
+
+    plan(keep[...], owner[...], me_z, meta, plan_rows)
+    to_scalars = pltpu.make_async_copy(plan_rows, planned, t_sem.at[0])
+    to_scalars.start()
+    to_scalars.wait()
     loads[0].wait()
     for part in range(halves):
         pack(part)
@@ -393,7 +414,7 @@
         chunk = keys[pl.ds(c * 4, 4)].reshape(1024, 128)
         kept_part = jnp.concatenate(
             [
-                jnp.where(jnp.full((1, 256), kept[c * 4 + part], I32) > 0, 0.0, FAR)
+                jnp.where(jnp.full((1, 256), planned[3, c * 4 + part], I32) > 0, 0.0, FAR)
                 for part in range(4)
             ],
             axis=1,
@@ -437,12 +458,12 @@
         return lambda i: buffer.at[lax.rem(me_lane + i, LANES)]
 
     settle(metas)
-    to_scalars = pltpu.make_async_copy(meta_ring, table, t_sem)
+    to_scalars = pltpu.make_async_copy(meta_ring, table, t_sem.at[1])
     to_scalars.start()
     to_scalars.wait()
-    out_meta[me_lane] = meta_ring[...]
+    meta_all[me_lane] = meta_ring[...]
     stats = share(plane_slice(stat_out), stat_plane, 0, me_lane, plane_peer, LANES)
-    metas = share(lambda i: meta_ring, out_meta, 5, me_lane, plane_peer, LANES)
+    metas = share(lambda i: meta_ring, meta_all, 5, me_lane, plane_peer, LANES)
 
     def merged(buffer):
         largest = buffer[0, 0:3, :]
@@ -463,11 +484,22 @@
         hand_on(part, 1)
         across(part, 1, 7)
     settle(metas)
-    most = out_meta[0, 0]
+    most = meta_all[0, 0]
     for lane in range(LANES):
         for z in range(NZ):
-            most = jnp.maximum(most, out_meta[lane, z])
+            most = jnp.maximum(most, meta_all[lane, z])
     needs_pair[me_b] = most
+    coded = jnp.concatenate(
+        [meta_all[lane, z] for z in range(NZ) for lane in range(LANES)], axis=0
+    ).astype(F32)
+    source = lax.broadcasted_iota(I32, (64, 128), 0)
+    lane_64 = lax.broadcasted_iota(I32, (64, 128), 1)
+    here = jnp.sum(jnp.where(lane_64 == me_lane, coded, 0.0), axis=1, keepdims=True) > 0.5
+    here = jnp.broadcast_to(jnp.where(here, 1.0, 0.0), (64, 128))
+    rank = jnp.dot(before_64(64), here.astype(BF16), preferred_element_type=F32)
+    chosen = (here > 0.5) & (jnp.abs(rank - lane_64.astype(F32)) < 0.5)
+    picks = jnp.sum(jnp.where(chosen, source.astype(F32), 0.0), axis=0, keepdims=True)
+    out_picks[...] = picks.astype(I32)
     pair = share(lambda i: needs_pair.at[me_b], needs_pair, 6, me_b, pair_peer, 2)
 
     settle(stats)
@@ -586,22 +618,6 @@
 ANY = pl.BlockSpec(memory_space=pl.ANY)
 
 
-def run_plan(keep, owner):
-    return pl.pallas_call(
-        plan,
-        out_shape=(
-            jax.ShapeDtypeStruct((2, SECOND), I32),
-            jax.ShapeDtypeStruct((LANES,), I32),
-            jax.ShapeDtypeStruct((BLOCKS,), I32),
-            jax.ShapeDtypeStruct((NZ, 128), I32),
-        ),
-        in_specs=[SMEM] * 2,
-        out_specs=(SMEM,) * 4,
-        scratch_shapes=[pltpu.SMEM((NZ * LANES,), I32)],
-        name="plan",
-    )(keep, owner)
-
-
 def run_exchange(slots, collective_id, scale2, operands):
     s1, s2, s3, s4 = slots
     block = (BLOCKS * 8, 128)
@@ -616,17 +632,20 @@
         out_shape=(
             jax.ShapeDtypeStruct((HEADS, BLOCKS * BLOCK), F32),
             jax.ShapeDtypeStruct((STEP_ROWS, 128), BF16),
-            jax.ShapeDtypeStruct((LANES, NZ, 1, 128), I32),
+            jax.ShapeDtypeStruct((1, 128), I32),
             jax.ShapeDtypeStruct((1,), I32),
             jax.ShapeDtypeStruct((NZ * LANES, *block), BF16),
             jax.ShapeDtypeStruct((NZ * LANES, *block), BF16),
         ),
-        in_specs=[SMEM] * 4 + [VMEM, ANY, ANY] + [VMEM] * 4,
+        in_specs=[SMEM, VMEM, VMEM, ANY, ANY] + [VMEM] * 4,
         out_specs=(VMEM,) * 3 + (SMEM,) + (ANY,) * 2,
         scratch_shapes=[
             pltpu.VMEM((BLOCKS, *block), BF16),
             pltpu.VMEM((BLOCKS, *block), BF16),
             pltpu.SemaphoreType.DMA((2,)),
+            pltpu.VMEM((NZ, 1, 128), I32),
+            pltpu.VMEM((8, 128), I32),
+            pltpu.SMEM((8, 128), I32),
             buffers(s1),
             buffers(s1),
             buffers(s1),
@@ -645,6 +664,7 @@
             pltpu.VMEM((8, STEP_ROWS, 1024), F32),
             pltpu.VMEM((HEADS, 16, WINDOW * GROUP), BF16),
             pltpu.VMEM((NZ, 1, 128), I32),
+            pltpu.VMEM((LANES, NZ, 1, 128), I32),
             pltpu.VMEM((2, 1, 128), I32),
             pltpu.SMEM((NZ, 1, 128), I32),
             *[pltpu.VMEM((8, 8, 128), F32)] * 4,
@@ -655,7 +675,7 @@
             pltpu.SemaphoreType.DMA((PARTS, NZ, LANES)),
             pltpu.SemaphoreType.DMA((10, 8)),
             pltpu.SemaphoreType.DMA((10, 8)),
-            pltpu.SemaphoreType.DMA,
+            pltpu.SemaphoreType.DMA((2,)),
         ],
         compiler_params=pltpu.CompilerParams(
             collective_id=collective_id,
@@ -667,21 +687,13 @@
 
 
 def unpack(
-    meta, scores, decoded, came_k, came_v, out_scores, out_decoded, out_k, out_v, held, picks, sems
+    picks, scores, decoded, came_k, came_v, out_scores, out_decoded, out_k, out_v, held, sems
 ):
-    me_lane = lax.axis_index("ctx_1") * 2 + lax.axis_index("ctx_2")
-
-    def choose(source, found):
-        z, lane = source // LANES, lax.rem(source, LANES)
-        picks[found] = source
-        return found + (meta[lane * NZ + z, me_lane] > 0).astype(I32)
-
-    lax.fori_loop(0, NZ * LANES, choose, 0)
     pairs = ((came_k, out_k), (came_v, out_v))
 
     def take(kind, j):
         return pltpu.make_async_copy(
-            pairs[kind][0].at[picks[j]], held.at[kind, j], sems.at[0, kind, j]
+            pairs[kind][0].at[picks[0, j]], held.at[kind, j], sems.at[0, kind, j]
         )
 
     def put(kind, j):
@@ -709,7 +721,7 @@
             put(kind, j).wait()
 
 
-def run_unpack(meta, scores, decoded, came_k, came_v):
+def run_unpack(picks, scores, decoded, came_k, came_v):
     block = came_k.shape[1:]
     shape = jax.ShapeDtypeStruct((KEEP, *block), BF16)
     return pl.pallas_call(
@@ -724,11 +736,10 @@
         out_specs=(VMEM, VMEM, ANY, ANY),
         scratch_shapes=[
             pltpu.VMEM((2, KEEP, *block), BF16),
-            pltpu.SMEM((NZ * LANES + 1,), I32),
             pltpu.SemaphoreType.DMA((2, 2, KEEP)),
         ],
         name="unpack",
-    )(meta.reshape(NZ * LANES, 128), scores, decoded, came_k, came_v)
+    )(picks, scores, decoded, came_k, came_v)
 
 
 def shards(
@@ -744,13 +755,10 @@
 ):
     tokens, head_count, width = stored_keys.shape
     scale2 = math.log2(math.e) / math.sqrt(width)
-    lists, own, kept, meta = run_plan(keep_lists, owner_ids)
     operands = (
-        lists,
-        own,
-        kept,
         cache_length,
-        meta.reshape(NZ, 1, 128),
+        keep_lists,
+        owner_ids,
         stored_keys.reshape(BLOCKS, BLOCK * head_count, width),
         stored_values.reshape(BLOCKS, BLOCK * head_count, width),
         observed_queries.transpose(1, 0, 2).reshape(HEADS, GROUP * WINDOW, width),
@@ -761,8 +769,8 @@
     first = run_exchange(FITS_MOST, 0, scale2, operands)
 
     def finish(result):
-        scores, decoded, came, _, came_k, came_v = result
-        return run_unpack(came, scores, decoded, came_k, came_v)
+        scores, decoded, picks, _, came_k, came_v = result
+        return run_unpack(picks, scores, decoded, came_k, came_v)
 
     scores, decoded, kept_keys, kept_values = lax.cond(
         first[3][0] > 0,

time: 166 us -> 162 us (0.976)
  Pallas kernels: 163 us -> 160 us
    pallas_call x1 -> x0, Pallas kernels: 1.98 us -> none  [run_plan(): pl.pallas_call(plan, out_shape=(jax.ShapeDtypeStruct((2, SECOND), I32), j...]
where the time goes in v5:
time: 162 us
  Pallas kernels  160 us (99%)
  between operations  2.13 us (1%)
    pallas_call x1, Pallas kernels, run_exchange(): pl.pallas_call(functools.partial(exchange, slots, scale2), out_shape=(jax...  154 us
    pallas_call x1, Pallas kernels, run_unpack(): pl.pallas_call(unpack, out_shape=(jax.ShapeDtypeStruct(scores.shape, scor...  5.58 us

profile of v5, /device:TPU:1, one launch (start us, length us, event | category | flops | bytes accessed | tf_op | source)
XLA Modules:
  0.0 161.9 jit_solution(18059853895219832990)
XLA Ops:
  1.3 154.0 %exchange_17.1 = (f32[4,2048]{1,0:T(4,128)}, bf16[80,128]{1,0:T(8,128)(2,1)}, s32[1,128]{1,0:T(1,128)}, s32[1]{0:T(128)}, bf16[64,256,128]{2,1,0:T(8,128)(2,1)}, /*index=5*/bf16[64,256,128]{2,1,0:T(8,128)(2,1)}) custom-call(s32[1]{0:T(128)S(6)} %copy.21.length, s32[1,26]{1,0:T(1,128)} %keep.1, s32[1,26]{1,0:T(1,128)} %owner.1, ...), custom_call_target="tpu_custom_call" | custom-call | tf_op jit(solution)/shard_map/exchange_17/pallas_call | solution.py:630
  156.0 5.8 %conditional.1 = ((f32[4,2048]{1,0:T(4,128)}, bf16[80,128]{1,0:T(8,128)(2,1)}, bf16[26,256,128]{2,1,0:T(8,128)(2,1)}, bf16[26,256,128]{2,1,0:T(8,128)(2,1)})) conditional(s32[]{:T(128)} %bitcast.8, (s32[1,128]{1,0:T(1,128)}, f32[4,2048]{1,0:T(4,128)}, bf16[80,128]{1,0:T(8,128)(2,1)}, bf16[64,256,128]{2,1,0:T(8,128)(2,1)}, ...), branch_computations={%region_0.0_spmd.clone, %region_1.0_spmd.clone} | conditional | bytes 8 | solution.py:775
  156.0 5.6 %unpack.4 = (f32[4,2048]{1,0:T(4,128)}, bf16[80,128]{1,0:T(8,128)(2,1)}, bf16[26,256,128]{2,1,0:T(8,128)(2,1)}, bf16[26,256,128]{2,1,0:T(8,128)(2,1)}) custom-call(s32[1,128]{1,0:T(1,128)} %get-tuple-element.105.picks, f32[4,2048]{1,0:T(4,128)} %get-tuple-element.106.scores, bf16[80,128]{1,0:T(8,128)(2,1)} %get-tuple-element.107.decoded, ...), custom_call_target="tpu_custom_call" | custom-call | tf_op jit(solution)/shard_map/cond/branch_0_fun/unpack/pallas_call | solution.py:727

commit v6 on v5

--- a/solution.py
+++ b/solution.py
@@ -123,7 +123,7 @@
     owner,
     keys_in,
     values_in,
-    queries,
+    queries_in,
     step_queries,
     new_keys,
     new_values,
@@ -135,6 +135,7 @@
     yr_v,
     keys,
     values,
+    queries,
     in_sem,
     meta,
     plan_rows,
@@ -198,7 +199,9 @@
 
     loads = [
         pltpu.make_async_copy(source, store, in_sem.at[kind])
-        for kind, (source, store) in enumerate(((keys_in, keys), (values_in, values)))
+        for kind, (source, store) in enumerate(
+            ((keys_in, keys), (values_in, values), (queries_in, queries))
+        )
     ]
     for load in loads:
         load.start()
@@ -233,8 +236,7 @@
     to_scalars.start()
     to_scalars.wait()
     loads[0].wait()
-    for part in range(halves):
-        pack(part)
+    pack(0)
     meta_ring[me_z] = meta[me_z]
     pl.semaphore_wait(barrier, LANES - 1 + NZ - 1 + 1)
 
@@ -347,7 +349,9 @@
                 ring_start(part, way, q, 1)
 
     every = range(HALF)
-    for part in range(halves):
+    ring_first(0, *every)
+    for part in range(1, halves):
+        pack(part)
         ring_first(part, *every)
     loads[1].wait()
     for part in range(halves, PARTS):
@@ -394,6 +398,7 @@
         redundancy[pl.ds(i, 1), :] = (row_sum - own_term) / jnp.maximum(in_block - 1.0, 1.0)
         return carry
 
+    loads[2].wait()
     lax.fori_loop(0, HEADS * 8, score, 0)
 
     row_of = lax.broadcasted_iota(I32, (STEP_ROWS, 128), 0)
@@ -637,12 +642,13 @@
             jax.ShapeDtypeStruct((NZ * LANES, *block), BF16),
             jax.ShapeDtypeStruct((NZ * LANES, *block), BF16),
         ),
-        in_specs=[SMEM, VMEM, VMEM, ANY, ANY] + [VMEM] * 4,
+        in_specs=[SMEM, VMEM, VMEM] + [ANY] * 3 + [VMEM] * 3,
         out_specs=(VMEM,) * 3 + (SMEM,) + (ANY,) * 2,
         scratch_shapes=[
             pltpu.VMEM((BLOCKS, *block), BF16),
             pltpu.VMEM((BLOCKS, *block), BF16),
-            pltpu.SemaphoreType.DMA((2,)),
+            pltpu.VMEM((HEADS, WINDOW * GROUP, 128), BF16),
+            pltpu.SemaphoreType.DMA((3,)),
             pltpu.VMEM((NZ, 1, 128), I32),
             pltpu.VMEM((8, 128), I32),
             pltpu.SMEM((8, 128), I32),

time: 162 us -> 162 us (level)
  no operation moved by 1% of the time
where the time goes in v6:
time: 162 us; the launch traced here: 161 us
  Pallas kernels  159 us (98%)
  between operations  2.13 us (1%)
    pallas_call x1, Pallas kernels, run_exchange(): pl.pallas_call(functools.partial(exchange, slots, scale2), out_shape=(jax...  154 us
    pallas_call x1, Pallas kernels, run_unpack(): pl.pallas_call(unpack, out_shape=(jax.ShapeDtypeStruct(scores.shape, scor...  5.58 us

profile of v6, /device:TPU:1, one launch (start us, length us, event | category | flops | bytes accessed | tf_op | source)
XLA Modules:
  0.0 161.4 jit_solution(3573474489237796857)
XLA Ops:
  1.3 153.5 %exchange_17.1 = (f32[4,2048]{1,0:T(4,128)}, bf16[80,128]{1,0:T(8,128)(2,1)}, s32[1,128]{1,0:T(1,128)}, s32[1]{0:T(128)}, bf16[64,256,128]{2,1,0:T(8,128)(2,1)}, /*index=5*/bf16[64,256,128]{2,1,0:T(8,128)(2,1)}) custom-call(s32[1]{0:T(128)S(6)} %copy.21.length, s32[1,26]{1,0:T(1,128)} %keep.1, s32[1,26]{1,0:T(1,128)} %owner.1, ...), custom_call_target="tpu_custom_call" | custom-call | tf_op jit(solution)/shard_map/exchange_17/pallas_call | solution.py:635
  155.5 5.8 %conditional.1 = ((f32[4,2048]{1,0:T(4,128)}, bf16[80,128]{1,0:T(8,128)(2,1)}, bf16[26,256,128]{2,1,0:T(8,128)(2,1)}, bf16[26,256,128]{2,1,0:T(8,128)(2,1)})) conditional(s32[]{:T(128)} %bitcast.8, (s32[1,128]{1,0:T(1,128)}, f32[4,2048]{1,0:T(4,128)}, bf16[80,128]{1,0:T(8,128)(2,1)}, bf16[64,256,128]{2,1,0:T(8,128)(2,1)}, ...), branch_computations={%region_0.0_spmd.clone, %region_1.0_spmd.clone} | conditional | bytes 8 | solution.py:781
  155.5 5.6 %unpack.4 = (f32[4,2048]{1,0:T(4,128)}, bf16[80,128]{1,0:T(8,128)(2,1)}, bf16[26,256,128]{2,1,0:T(8,128)(2,1)}, bf16[26,256,128]{2,1,0:T(8,128)(2,1)}) custom-call(s32[1,128]{1,0:T(1,128)} %get-tuple-element.105.picks, f32[4,2048]{1,0:T(4,128)} %get-tuple-element.106.scores, bf16[80,128]{1,0:T(8,128)(2,1)} %get-tuple-element.107.decoded, ...), custom_call_target="tpu_custom_call" | custom-call | tf_op jit(solution)/shard_map/cond/branch_0_fun/unpack/pallas_call | solution.py:733

commit v7 on v6

--- a/solution.py
+++ b/solution.py
@@ -30,7 +30,7 @@
 BLOCKS = 32
 SECOND = 32
 FITS_ALL = (26, 20, 12, 4)
-FITS_MOST = (17, 13, 10, 4)
+FITS_MOST = (17, 13, 9, 4)
 F32, BF16, I32 = jnp.float32, jnp.bfloat16, jnp.int32
 
 
@@ -62,7 +62,7 @@
     return jnp.sum(jnp.where(same, block, 0.0), axis=0, keepdims=True)
 
 
-def plan(keep, owner, me_z, meta, lists):
+def plan(slots, keep, owner, me_z, meta, lists):
     ahead_of_me = (owner + (NZ - me_z) * LANES) & (NZ * LANES - 1)
     match = lax.broadcasted_iota(I32, (NZ * LANES, KEEP), 0) == ahead_of_me
     wide = (NZ * LANES, 128)
@@ -79,7 +79,15 @@
     n4 = count[HALF]
     ahead, behind = count[1] + count[2] + count[3], count[7] + count[6] + count[5]
     even = jnp.maximum(jnp.floor((n4 + behind - ahead + 1.0) * 0.5), 0.0)
-    first = jnp.maximum(jnp.maximum(n4 - 4.0, 0.0), jnp.minimum(jnp.minimum(n4, 4.0), even))
+
+    def room(three, two, near):
+        return jnp.minimum(
+            jnp.minimum(slots[2] - three, slots[1] - three - two), slots[0] - three - two - near
+        )
+
+    first = jnp.maximum(even, n4 - room(count[5], count[6], count[7]))
+    first = jnp.minimum(first, room(count[3], count[2], count[1]))
+    first = jnp.maximum(jnp.maximum(n4 - 4.0, 0.0), jnp.minimum(jnp.minimum(n4, 4.0), first))
     second = n4 - first
     tails_p = [first, first + count[3], first + count[3] + count[2], first + ahead]
     tails_m = [second, second + count[5], second + count[5] + count[6], second + behind]
@@ -231,7 +239,7 @@
         for i in range(LANES):
             yb[part, 0, i] = store[block_at(2, lax.rem(me_lane + i, LANES)), rows]
 
-    plan(keep[...], owner[...], me_z, meta, plan_rows)
+    plan(slots, keep[...], owner[...], me_z, meta, plan_rows)
     to_scalars = pltpu.make_async_copy(plan_rows, planned, t_sem.at[0])
     to_scalars.start()
     to_scalars.wait()

time: 162 us -> 159 us (0.981)
  Pallas kernels: 159 us -> 156 us
    pallas_call x1, Pallas kernels: 154 us -> 151 us  [run_exchange(): pl.pallas_call(functools.partial(exchange, slots, scale2), out_shape=(jax...]
where the time goes in v7:
time: 159 us
  Pallas kernels  156 us (98%)
  between operations  2.13 us (1%)
    pallas_call x1, Pallas kernels, run_exchange(): pl.pallas_call(functools.partial(exchange, slots, scale2), out_shape=(jax...  151 us
    pallas_call x1, Pallas kernels, run_unpack(): pl.pallas_call(unpack, out_shape=(jax.ShapeDtypeStruct(scores.shape, scor...  5.58 us

profile of v7, /device:TPU:1, one launch (start us, length us, event | category | flops | bytes accessed | tf_op | source)
XLA Modules:
  0.0 158.6 jit_solution(14102579680956146630)
XLA Ops:
  1.3 150.7 %exchange_17.1 = (f32[4,2048]{1,0:T(4,128)}, bf16[80,128]{1,0:T(8,128)(2,1)}, s32[1,128]{1,0:T(1,128)}, s32[1]{0:T(128)}, bf16[64,256,128]{2,1,0:T(8,128)(2,1)}, /*index=5*/bf16[64,256,128]{2,1,0:T(8,128)(2,1)}) custom-call(s32[1]{0:T(128)S(6)} %copy.21.length, s32[1,26]{1,0:T(1,128)} %keep.1, s32[1,26]{1,0:T(1,128)} %owner.1, ...), custom_call_target="tpu_custom_call" | custom-call | tf_op jit(solution)/shard_map/exchange_17/pallas_call | solution.py:643
  152.7 5.8 %conditional.1 = ((f32[4,2048]{1,0:T(4,128)}, bf16[80,128]{1,0:T(8,128)(2,1)}, bf16[26,256,128]{2,1,0:T(8,128)(2,1)}, bf16[26,256,128]{2,1,0:T(8,128)(2,1)})) conditional(s32[]{:T(128)} %bitcast.8, (s32[1,128]{1,0:T(1,128)}, f32[4,2048]{1,0:T(4,128)}, bf16[80,128]{1,0:T(8,128)(2,1)}, bf16[64,256,128]{2,1,0:T(8,128)(2,1)}, ...), branch_computations={%region_0.0_spmd.clone, %region_1.0_spmd.clone} | conditional | bytes 8 | solution.py:789
  152.7 5.6 %unpack.4 = (f32[4,2048]{1,0:T(4,128)}, bf16[80,128]{1,0:T(8,128)(2,1)}, bf16[26,256,128]{2,1,0:T(8,128)(2,1)}, bf16[26,256,128]{2,1,0:T(8,128)(2,1)}) custom-call(s32[1,128]{1,0:T(1,128)} %get-tuple-element.105.picks, f32[4,2048]{1,0:T(4,128)} %get-tuple-element.106.scores, bf16[80,128]{1,0:T(8,128)(2,1)} %get-tuple-element.107.decoded, ...), custom_call_target="tpu_custom_call" | custom-call | tf_op jit(solution)/shard_map/cond/branch_0_fun/unpack/pallas_call | solution.py:741
